TPU v7x, 512 devices: a whole 4x4x16 slice. The times are simulated.
512 devices in a mesh: orb: 16 (over z), space: 32 (over y, x, core).
Axes of the slice: x: 4, y: 4, z: 16, core: 2. Of those that a mesh axis runs over, the one named last changes fastest.
Arguments:
- orbitals: float32 [32, 512, 128], P('orb', 'space'), may hold values from 0 to 0.25
- points: float32 [3, 512, 128], P(None, 'space')
- quad_weight: float32 [512, 128], P('space'), may hold values from 0.5 to 2
- external: float32 [512, 128], P('space'), may hold values from -3 to 1
- screening: float32 [32], replicated, may hold values from 0.05 to 2
- level_index: int32 [32], P('orb'), may hold values from 0 to 31
- near_cells: int32 [512, 27], P('space'), may hold values from -1 to 511, as said below
- far_cells: int32 [512, 42], P('space'), may hold values from -1 to 511, as said below
Outputs:
- new_orbitals: float32 [32, 512, 128], P('orb', 'space')
- hartree: float32 [512, 128], P('space')
Inputs may be any that keep to these rules, and one draw needn't show every extreme that they name: `near_cells`: row t lists distinct cells in increasing order, then -1: every cell of its own plane whose first two box indices differ from those of t by at most one (t itself among them), the cells directly above and below t, and some of the other cells of the two adjacent planes whose first two box indices differ from those of t by at most one. Some row holds 27 cells. `far_cells`: row t lists in increasing order, then -1, all cells of the planes floor(t / 16) - 1 to floor(t / 16) + 1 that are not in row t of near_cells. Some row holds 42 cells.
All inputs are finite; a program needn't handle non-finite values.
Results may differ from a plain program's by a relative error of at most 0.0003.
Values sent between devices are 32-bit elements; how exact they have to be, the bound alone decides.
A program may use at most 64 MiB of HBM per device.

v0:
```python
import math

import jax
import jax.numpy as jnp
from jax import lax
from jax.sharding import PartitionSpec as P

NODES = 4


cell_side = 0.25
soften = 6.25e-06
green_scale = -0.5 / math.pi


def padded(cells, sides, width):
    for axis, dim in sides:
        count = lax.axis_size(axis)
        ends = count - 1
        head = lax.slice_in_dim(cells, 0, width, axis=dim)
        tail = lax.slice_in_dim(cells, cells.shape[dim] - width, cells.shape[dim], axis=dim)
        cells = jnp.concatenate(
            [
                lax.ppermute(tail, axis, [(i, (i + 1) % count) for i in range(ends)]),
                cells,
                lax.ppermute(head, axis, [((i + 1) % count, i) for i in range(ends)]),
            ],
            axis=dim,
        )
    return cells


def cheb_nodes(node_count):
    indices = jnp.arange(node_count, dtype=jnp.int32).astype(jnp.float32)
    return jnp.cos((2.0 * indices + 1.0) * (math.pi / (2.0 * node_count)))


def lagrange(scaled, node_set, node_count):
    factors = []
    for outer_node in range(node_count):
        running = jnp.ones_like(scaled)
        for inner_node in range(node_count):
            if inner_node != outer_node:
                running = running * (
                    (scaled - node_set[inner_node]) / (node_set[outer_node] - node_set[inner_node])
                )
        factors.append(running)
    return jnp.stack(factors)


def anterp(locations, corners, extent):
    node_set = cheb_nodes(NODES)
    scaled = 2.0 * (locations - corners[:, :, None]) / extent[:, None, None] - 1.0
    basis_x = lagrange(scaled[0], node_set, NODES)
    basis_y = lagrange(scaled[1], node_set, NODES)
    basis_z = lagrange(scaled[2], node_set, NODES)
    weights = basis_x[:, None, None] * basis_y[None, :, None] * basis_z[None, None, :]
    return weights.reshape((NODES * NODES * NODES,) + locations.shape[1:])


def proxies(corners, extent):
    node_set = cheb_nodes(NODES)
    offset = 0.5 * (node_set + 1.0)
    grid_shape = (NODES, NODES, NODES) + corners.shape[1:]
    grid_x = jnp.broadcast_to(
        (corners[0][None, :] + offset[:, None] * extent[0])[:, None, None], grid_shape
    )
    grid_y = jnp.broadcast_to(
        (corners[1][None, :] + offset[:, None] * extent[1])[None, :, None], grid_shape
    )
    grid_z = jnp.broadcast_to(
        (corners[2][None, :] + offset[:, None] * extent[2])[None, None, :], grid_shape
    )
    stacked = jnp.stack([grid_x, grid_y, grid_z]).reshape(
        (3, NODES * NODES * NODES) + corners.shape[1:]
    )
    return jnp.moveaxis(stacked, 1, 2)


def cell_lows(cell_ids):
    return (
        jnp.stack([cell_ids % 4, cell_ids // 4 % 4, cell_ids // 16]).astype(jnp.float32) * cell_side
    )


def plane_lows(levels):
    zeroes = jnp.zeros_like(levels)
    return jnp.stack([zeroes, zeroes, levels]).astype(jnp.float32) * cell_side


def cell_extent():
    return jnp.full((3,), cell_side, jnp.float32)


def plane_extent():
    return jnp.array([4.0 * cell_side, 4.0 * cell_side, cell_side], jnp.float32)


def kernel_sum(targets, locations, values, decay_rates):
    squared = jnp.zeros((targets.shape[1], locations.shape[1]), jnp.float32)
    for component in range(3):
        difference = targets[component][:, None] - locations[component][None, :]
        squared = squared + difference * difference
    distance = jnp.sqrt(squared + soften)
    kernel = jnp.exp(-decay_rates[:, None, None] * distance[None]) / distance[None]
    return jnp.sum(kernel * values[:, None, :], axis=2)


def cell_moments(mapping, values):
    return jnp.einsum("pcj,rcj->rcp", mapping, values, precision=lax.Precision.HIGHEST)


def plane_moments(mapping, values):
    grouped = values.reshape(values.shape[0], mapping.shape[1], -1)
    return jnp.einsum("pgj,rgj->rgp", mapping, grouped, precision=lax.Precision.HIGHEST)


def evaluate(
    targets,
    first_cell,
    target_offset,
    rim_points,
    rim_values,
    rim_mom,
    plane_proxy,
    plane_mom,
    near_cells,
    far_cells,
    decay_rates,
):
    kinds = rim_values.shape[0]
    levels = jnp.arange(plane_mom.shape[1], dtype=jnp.int32)
    extent = cell_extent()
    rim_base = first_cell - 16

    def per_cell(index):
        near_ids = near_cells[index]
        near_live = (near_ids >= 0).astype(jnp.float32)
        near_slot = jnp.where(near_ids >= 0, near_ids - rim_base, 0)
        near_src = rim_points[:, near_slot, :].reshape(3, -1)
        near_val = (rim_values[:, near_slot, :] * near_live[None, :, None]).reshape(kinds, -1)
        far_ids = far_cells[index]
        far_live = (far_ids >= 0).astype(jnp.float32)
        far_slot = jnp.where(far_ids >= 0, far_ids - rim_base, 0)
        far_src = proxies(cell_lows(jnp.maximum(far_ids, 0)), extent).reshape(3, -1)
        far_val = (rim_mom[:, far_slot, :] * far_live[None, :, None]).reshape(kinds, -1)
        plane_keep = (jnp.abs(levels - (first_cell + target_offset + index) // 16) >= 2).astype(
            jnp.float32
        )
        coarse_val = (plane_mom * plane_keep[None, :, None]).reshape(kinds, -1)
        points_here = targets[:, index, :]
        return (
            kernel_sum(points_here, near_src, near_val, decay_rates)
            + kernel_sum(points_here, far_src, far_val, decay_rates)
            + kernel_sum(points_here, plane_proxy, coarse_val, decay_rates)
        )

    count = targets.shape[1]
    group = 2 if count % 2 == 0 else 1
    grouped = jnp.arange(count, dtype=jnp.int32).reshape(count // group, group)
    result = lax.map(jax.vmap(per_cell), grouped)
    return result.reshape((count,) + result.shape[2:])


def body(orbitals, points, quad_weight, external, screening, level_index, near_cells, far_cells):
    cell_dev = orbitals.shape[1]
    point_count = orbitals.shape[2]
    spaces = lax.axis_size("space")
    first_cell = lax.axis_index("space") * cell_dev
    plane_dev = cell_dev // 16
    planes = plane_dev * spaces
    weight = quad_weight * (cell_side**3 / point_count)
    partial_value = 2.0 * jnp.sum(orbitals * orbitals, axis=0)
    density = lax.psum(partial_value, "orb")
    own_ids = first_cell + jnp.arange(cell_dev, dtype=jnp.int32)
    cell_map = anterp(points, cell_lows(own_ids), cell_extent())
    own_levels = first_cell // 16 + jnp.arange(plane_dev, dtype=jnp.int32)
    plane_map = anterp(points.reshape(3, plane_dev, -1), plane_lows(own_levels), plane_extent())
    levels = jnp.arange(planes, dtype=jnp.int32)
    plane_proxy = proxies(plane_lows(levels), plane_extent()).reshape(3, -1)
    charge = (weight * density)[None]
    charge_mom = cell_moments(cell_map, charge)
    charge_plane = plane_moments(plane_map, charge)
    rim_points, rim_charge, rim_charge_mom = (
        padded(points, (("space", 1),), 16),
        padded(charge, (("space", 1),), 16),
        padded(charge_mom, (("space", 1),), 16),
    )
    all_charge_planes = lax.all_gather(charge_plane, "space", axis=1, tiled=True)
    no_decay = jnp.zeros((1,), jnp.float32)
    share_cells = cell_dev // lax.axis_size("orb")
    share_start = lax.axis_index("orb") * share_cells
    targets = lax.dynamic_slice_in_dim(points, share_start, share_cells, 1)
    near_share = lax.dynamic_slice_in_dim(near_cells, share_start, share_cells, 0)
    far_share = lax.dynamic_slice_in_dim(far_cells, share_start, share_cells, 0)
    partial_field = evaluate(
        targets,
        first_cell,
        share_start,
        rim_points,
        rim_charge,
        rim_charge_mom,
        plane_proxy,
        all_charge_planes,
        near_share,
        far_share,
        no_decay,
    )[:, 0, :]
    hartree = lax.all_gather(partial_field, "orb", axis=0, tiled=True)
    potential = external + hartree
    sources = (weight * potential)[None] * orbitals
    source_mom = cell_moments(cell_map, sources)
    source_plane = plane_moments(plane_map, sources)
    rim_sources, rim_source_mom = (
        padded(sources, (("space", 1),), 16),
        padded(source_mom, (("space", 1),), 16),
    )
    all_source_planes = lax.all_gather(source_plane, "space", axis=1, tiled=True)
    level_match = (
        level_index[:, None] == jnp.arange(screening.shape[0], dtype=jnp.int32)[None, :]
    ).astype(jnp.float32)
    decay_rates = jnp.sum(level_match * screening[None, :], axis=1)
    updated = green_scale * evaluate(
        points,
        first_cell,
        0,
        rim_points,
        rim_sources,
        rim_source_mom,
        plane_proxy,
        all_source_planes,
        near_cells,
        far_cells,
        decay_rates,
    )
    return (jnp.transpose(updated, (1, 0, 2)), hartree)


def solution(mesh):
    in_specs = (
        P("orb", "space", None),
        P(None, "space", None),
        P("space", None),
        P("space", None),
        P(),
        P("orb"),
        P("space", None),
        P("space", None),
    )
    out_specs = (P("orb", "space", None), P("space", None))
    return jax.shard_map(body, mesh=mesh, in_specs=in_specs, out_specs=out_specs, check_vma=False)
```

profile of v0, /device:TPU:1, one launch (start us, length us, event | category | flops | bytes accessed | tf_op | source)
XLA Modules:
  0.0 432.9 jit_solution(6223612535126471700)
XLA Ops:
  20.1 2.7 divide_multiply_fusion.35
  22.8 2.7 divide_multiply_fusion.32
  26.3 30.8 %psum.7 = f32[16,128]{1,0:T(8,128)S(1)} all-reduce(f32[16,128]{1,0:T(8,128)S(1)} %broadcast_multiply_fusion.8), channel_id=1, replica_groups=mesh['orb'=16,'space'=32] {'orb'}, use_global_device_ids=true, to_apply=%region_1.0 | all-reduce | flops 2048 | bytes 16384 | tf_op jit(solution)/shard_map/psum | solution.py:174
  58.8 10.9 %collective-permute-start.4 = (f32[1,16,64]{2,1,0:T(8,128)S(1)}, f32[1,16,64]{2,1,0:T(8,128)S(1)}, u32[]{:S(2)}, u32[]{:S(2)}) collective-permute-start(f32[1,16,64]{2,1,0:T(8,128)S(1)} %bitcast.320), channel_id=1, source_target_pairs={{0,1},{1,2},{2,3},{3,4},{4,5},{5,6},{6,7},{7,8},{8,9},{9,10},{10,1... | collective-permute-start | bytes 12296 | tf_op jit(solution)/shard_map/ppermute | solution.py:24
  71.6 3.6 collective-permute-start.2
  77.9 3.6 collective-permute-start
  82.5 2.7 divide_multiply_fusion.22
  85.2 2.7 divide_multiply_fusion.18
  92.6 62.1 %all-reduce.2 = f32[2048]{0:T(1024)S(1)} all-reduce(f32[2048]{0:T(1024)S(1)} %dynamic-update-slice), channel_id=2, replica_groups=mesh['orb'=16,'space'=32] {'space'}, use_global_device_ids=true, to_apply=%add.2 | all-reduce | flops 2048 | bytes 16384
  157.9 5.3 %collective-permute-start.1 = (f32[3,16,128]{2,0,1:T(4,128)}, f32[3,16,128]{2,0,1:T(4,128)S(1)}, u32[]{:S(2)}, u32[]{:S(2)}) collective-permute-start(f32[3,16,128]{2,0,1:T(4,128)} %copy.89), channel_id=1, source_target_pairs={{1,0},{2,1},{3,2},{4,3},{5,4},{6,5},{7,6},{8,7},{9,8},{10,9},{11,1... | collective-permute-start | bytes 73736 | tf_op jit(solution)/shard_map/ppermute | solution.py:26
  167.9 19.0 %all-gather.3 = f32[16,1,128]{2,1,0:T(1,128)S(1)} all-gather(f32[1,1,128]{2,1,0:T(1,128)S(1)} %add_bitcast_fusion), channel_id=3, replica_groups=mesh['orb'=16,'space'=32] {'orb'}, dimensions={0}, use_global_device_ids=true | all-gather | bytes 8704 | tf_op jit(solution)/shard_map/all_gather | solution.py:209
  188.4 7.2 %collective-permute-start.8 = (f32[2,16,64]{2,0,1:T(2,128)S(1)}, f32[2,16,64]{2,0,1:T(2,128)S(1)}, u32[]{:S(2)}, u32[]{:S(2)}) collective-permute-start(f32[2,16,64]{2,0,1:T(2,128)S(1)} %convolution_bitcast_fusion), channel_id=1, source_target_pairs={{0,1},{1,2},{2,3},{3,4},{4,5},{5,6},{6,7},{7,8},{8,9},{9,10},{10,1... | collective-permute-start | bytes 24584 | tf_op jit(solution)/shard_map/ppermute | solution.py:24
  195.7 2.3 collective-permute-start.9
  198.5 3.3 collective-permute-start.6
  203.7 27.2 %all-gather.4 = f32[32,64,2]{1,2,0:T(2,128)S(1)} all-gather(f32[1,64,2]{1,2,0:T(2,128)S(1)} %convolution_bitcast_fusion.1), channel_id=4, replica_groups=mesh['orb'=16,'space'=32] {'space'}, dimensions={0}, use_global_device_ids=true | all-gather | bytes 16896 | tf_op jit(solution)/shard_map/all_gather | solution.py:218
  232.4 197.8 %while.19 = (s32[]{:T(128)}, f32[8,2,2,128]{3,2,1,0:T(2,128)}, f32[1,2,1,1]{1,3,2,0:T(1,128)S(1)}, s32[8,2]{1,0:T(8,128)}, f32[3,16,128]{2,0,1:T(4,128)}, /*inde...) while((s32[]{:T(128)}, f32[8,2,2,128]{3,2,1,0:T(2,128)}, ...), condition=%wide.wide.region_10.11_spmd.clone, body=%wide.wide.region_6.10_spmd.clone.sunk | while | flops 35724108 | bytes 20266744 | solution.py:161
  242.9 3.2 add_sqrt_fusion.10
  249.9 3.2 multiply_reduce_fusion.14
  267.7 3.2 add_sqrt_fusion.10
  274.6 3.2 multiply_reduce_fusion.14
  292.4 3.2 add_sqrt_fusion.10
  299.3 3.2 multiply_reduce_fusion.14
  317.1 3.2 add_sqrt_fusion.10
  324.1 3.2 multiply_reduce_fusion.14
  341.9 3.2 add_sqrt_fusion.10
  348.8 3.2 multiply_reduce_fusion.14
  366.6 3.2 add_sqrt_fusion.10
  373.5 3.2 multiply_reduce_fusion.14
  391.3 3.2 add_sqrt_fusion.10
  398.3 3.2 multiply_reduce_fusion.14
  416.1 3.2 add_sqrt_fusion.10
  423.0 3.2 multiply_reduce_fusion.14
  (839 shorter events, 174.6 us)
Async XLA Ops:
  0.6 81.8 %copy-start.25 = (f32[3]{0:T(128)S(1)}, f32[3]{0:T(128)}, u32[]{:S(2)}) copy-start(f32[3]{0:T(128)} %constant.413) | copy-start | bytes 40
  0.6 76.6 %copy-start.11 = (f32[3,16,128]{2,1,0:T(8,128)S(1)}, f32[3,16,128]{2,1,0:T(8,128)}, u32[]{:S(2)}) copy-start(f32[3,16,128]{2,1,0:T(8,128)} %param.13) | copy-start | bytes 73732
  0.7 87.4 %copy-start.14 = (s32[16,27]{1,0:T(8,128)S(1)}, s32[16,27]{1,0:T(8,128)}, u32[]{:S(2)}) copy-start(s32[16,27]{1,0:T(8,128)} %param.18) | copy-start | bytes 5188
  58.8 96.1 %copy-start.26 = (f32[32]{0:T(128)S(1)}, f32[32]{0:T(128)}, u32[]{:S(2)}) copy-start(f32[32]{0:T(128)} %constant.394.clone.1) | copy-start | bytes 388
  58.8 99.0 %collective-permute-start.4 = (f32[1,16,64]{2,1,0:T(8,128)S(1)}, f32[1,16,64]{2,1,0:T(8,128)S(1)}, u32[]{:S(2)}, u32[]{:S(2)}) collective-permute-start(f32[1,16,64]{2,1,0:T(8,128)S(1)} %bitcast.320), channel_id=1, source_target_pairs={{0,1},{1,2},{2,3},{3,4},{4,5},{5,6},{6,7},{7,8},{8,9},{9,10},{10,1... | collective-permute-start | bytes 12296 | tf_op jit(solution)/shard_map/ppermute | solution.py:24
  69.7 93.4 %collective-permute-start.5 = (f32[1,16,64]{2,1,0:T(8,128)S(1)}, f32[1,16,64]{2,1,0:T(8,128)S(1)}, u32[]{:S(2)}, u32[]{:S(2)}) collective-permute-start(f32[1,16,64]{2,1,0:T(8,128)S(1)} %bitcast.321), channel_id=1, source_target_pairs={{1,0},{2,1},{3,2},{4,3},{5,4},{6,5},{7,6},{8,7},{9,8},{10,9},{11,1... | collective-permute-start | bytes 12296 | tf_op jit(solution)/shard_map/ppermute | solution.py:26
  71.6 93.4 %collective-permute-start.2 = (f32[1,16,128]{2,1,0:T(8,128)S(1)}, f32[1,16,128]{2,1,0:T(8,128)S(1)}, u32[]{:S(2)}, u32[]{:S(2)}) collective-permute-start(f32[1,16,128]{2,1,0:T(8,128)S(1)} %bitcast.310), channel_id=1, source_target_pairs={{0,1},{1,2},{2,3},{3,4},{4,5},{5,6},{6,7},{7,8},{8,9},{9,10},{10,1... | collective-permute-start | bytes 24584 | tf_op jit(solution)/shard_map/ppermute | solution.py:24
  75.3 89.7 %collective-permute-start.3 = (f32[1,16,128]{2,1,0:T(8,128)S(1)}, f32[1,16,128]{2,1,0:T(8,128)S(1)}, u32[]{:S(2)}, u32[]{:S(2)}) collective-permute-start(f32[1,16,128]{2,1,0:T(8,128)S(1)} %bitcast.311), channel_id=1, source_target_pairs={{1,0},{2,1},{3,2},{4,3},{5,4},{6,5},{7,6},{8,7},{9,8},{10,9},{11,1... | collective-permute-start | bytes 24584 | tf_op jit(solution)/shard_map/ppermute | solution.py:26
  77.9 87.8 %collective-permute-start = (f32[3,16,128]{2,0,1:T(4,128)}, f32[3,16,128]{2,0,1:T(4,128)S(1)}, u32[]{:S(2)}, u32[]{:S(2)}) collective-permute-start(f32[3,16,128]{2,0,1:T(4,128)} %copy.89), channel_id=1, source_target_pairs={{0,1},{1,2},{2,3},{3,4},{4,5},{5,6},{6,7},{7,8},{8,9},{9,10},{10,1... | collective-permute-start | bytes 73736 | tf_op jit(solution)/shard_map/ppermute | solution.py:24
  89.0 66.8 %copy-start.27 = (f32[32]{0:T(128)S(1)}, f32[32]{0:T(128)}, u32[]{:S(2)}) copy-start(f32[32]{0:T(128)} %param.16) | copy-start | bytes 388
  89.0 66.8 %copy-start.28 = (s32[2]{0:T(128)S(1)}, s32[2]{0:T(128)}, u32[]{:S(2)}) copy-start(s32[2]{0:T(128)} %param.17) | copy-start | bytes 28
  157.9 7.8 %collective-permute-start.1 = (f32[3,16,128]{2,0,1:T(4,128)}, f32[3,16,128]{2,0,1:T(4,128)S(1)}, u32[]{:S(2)}, u32[]{:S(2)}) collective-permute-start(f32[3,16,128]{2,0,1:T(4,128)} %copy.89), channel_id=1, source_target_pairs={{1,0},{2,1},{3,2},{4,3},{5,4},{6,5},{7,6},{8,7},{9,8},{10,9},{11,1... | collective-permute-start | bytes 73736 | tf_op jit(solution)/shard_map/ppermute | solution.py:26
  163.8 23.6 %copy-start.23 = (f32[16,128]{1,0:T(8,128)S(1)}, f32[16,128]{1,0:T(8,128)}, u32[]{:S(2)}) copy-start(f32[16,128]{1,0:T(8,128)} %param.14) | copy-start | bytes 24580
  163.8 23.6 %copy-start.24 = (f32[16,128]{1,0:T(8,128)S(1)}, f32[16,128]{1,0:T(8,128)}, u32[]{:S(2)}) copy-start(f32[16,128]{1,0:T(8,128)} %param.15) | copy-start | bytes 24580
  163.8 23.6 %copy-start.22 = (f32[2,16,128]{2,1,0:T(8,128)S(1)}, f32[2,16,128]{2,1,0:T(8,128)}, u32[]{:S(2)}) copy-start(f32[2,16,128]{2,1,0:T(8,128)} %param.12) | copy-start | bytes 49156
  188.4 42.8 %collective-permute-start.8 = (f32[2,16,64]{2,0,1:T(2,128)S(1)}, f32[2,16,64]{2,0,1:T(2,128)S(1)}, u32[]{:S(2)}, u32[]{:S(2)}) collective-permute-start(f32[2,16,64]{2,0,1:T(2,128)S(1)} %convolution_bitcast_fusion), channel_id=1, source_target_pairs={{0,1},{1,2},{2,3},{3,4},{4,5},{5,6},{6,7},{7,8},{8,9},{9,10},{10,1... | collective-permute-start | bytes 24584 | tf_op jit(solution)/shard_map/ppermute | solution.py:24
  195.7 36.1 %collective-permute-start.9 = (f32[2,16,64]{2,0,1:T(2,128)S(1)}, f32[2,16,64]{2,0,1:T(2,128)S(1)}, u32[]{:S(2)}, u32[]{:S(2)}) collective-permute-start(f32[2,16,64]{2,0,1:T(2,128)S(1)} %convolution_bitcast_fusion), channel_id=1, source_target_pairs={{1,0},{2,1},{3,2},{4,3},{5,4},{6,5},{7,6},{8,7},{9,8},{10,9},{11,1... | collective-permute-start | bytes 24584 | tf_op jit(solution)/shard_map/ppermute | solution.py:26
  198.5 33.3 %collective-permute-start.6 = (f32[2,16,128]{2,0,1:T(2,128)S(1)}, f32[2,16,128]{2,0,1:T(2,128)S(1)}, u32[]{:S(2)}, u32[]{:S(2)}) collective-permute-start(f32[2,16,128]{2,0,1:T(2,128)S(1)} %copy_multiply_fusion), channel_id=1, source_target_pairs={{0,1},{1,2},{2,3},{3,4},{4,5},{5,6},{6,7},{7,8},{8,9},{9,10},{10,1... | collective-permute-start | bytes 49160 | tf_op jit(solution)/shard_map/ppermute | solution.py:24
  201.8 30.0 %collective-permute-start.7 = (f32[2,16,128]{2,0,1:T(2,128)S(1)}, f32[2,16,128]{2,0,1:T(2,128)S(1)}, u32[]{:S(2)}, u32[]{:S(2)}) collective-permute-start(f32[2,16,128]{2,0,1:T(2,128)S(1)} %copy_multiply_fusion), channel_id=1, source_target_pairs={{1,0},{2,1},{3,2},{4,3},{5,4},{6,5},{7,6},{8,7},{9,8},{10,9},{11,1... | collective-permute-start | bytes 49160 | tf_op jit(solution)/shard_map/ppermute | solution.py:26
  232.4 9.8 %copy-start.2 = (f32[3,48,128]{2,0,1:T(4,128)}, f32[3,48,128]{2,0,1:T(4,128)S(1)}, u32[]{:S(2)}) copy-start(f32[3,48,128]{2,0,1:T(4,128)S(1)} %get-tuple-element.745) | copy-start | bytes 221188 | tf_op jit(solution)/shard_map/while
  257.1 7.2 %copy-start.19 = (f32[1,2,1,1]{1,3,2,0:T(1,128)}, f32[1,2,1,1]{1,3,2,0:T(1,128)S(1)}, u32[]{:S(2)}) copy-start(f32[1,2,1,1]{1,3,2,0:T(1,128)S(1)} %get-tuple-element.740) | copy-start | bytes 28 | tf_op jit(solution)/shard_map/while
  257.1 9.8 %copy-start.2 = (f32[3,48,128]{2,0,1:T(4,128)}, f32[3,48,128]{2,0,1:T(4,128)S(1)}, u32[]{:S(2)}) copy-start(f32[3,48,128]{2,0,1:T(4,128)S(1)} %get-tuple-element.745) | copy-start | bytes 221188 | tf_op jit(solution)/shard_map/while
  281.8 9.8 %copy-start.2 = (f32[3,48,128]{2,0,1:T(4,128)}, f32[3,48,128]{2,0,1:T(4,128)S(1)}, u32[]{:S(2)}) copy-start(f32[3,48,128]{2,0,1:T(4,128)S(1)} %get-tuple-element.745) | copy-start | bytes 221188 | tf_op jit(solution)/shard_map/while
  306.6 9.8 %copy-start.2 = (f32[3,48,128]{2,0,1:T(4,128)}, f32[3,48,128]{2,0,1:T(4,128)S(1)}, u32[]{:S(2)}) copy-start(f32[3,48,128]{2,0,1:T(4,128)S(1)} %get-tuple-element.745) | copy-start | bytes 221188 | tf_op jit(solution)/shard_map/while
  331.3 7.2 %copy-start.19 = (f32[1,2,1,1]{1,3,2,0:T(1,128)}, f32[1,2,1,1]{1,3,2,0:T(1,128)S(1)}, u32[]{:S(2)}) copy-start(f32[1,2,1,1]{1,3,2,0:T(1,128)S(1)} %get-tuple-element.740) | copy-start | bytes 28 | tf_op jit(solution)/shard_map/while
  331.3 9.8 %copy-start.2 = (f32[3,48,128]{2,0,1:T(4,128)}, f32[3,48,128]{2,0,1:T(4,128)S(1)}, u32[]{:S(2)}) copy-start(f32[3,48,128]{2,0,1:T(4,128)S(1)} %get-tuple-element.745) | copy-start | bytes 221188 | tf_op jit(solution)/shard_map/while
  356.0 7.2 %copy-start.19 = (f32[1,2,1,1]{1,3,2,0:T(1,128)}, f32[1,2,1,1]{1,3,2,0:T(1,128)S(1)}, u32[]{:S(2)}) copy-start(f32[1,2,1,1]{1,3,2,0:T(1,128)S(1)} %get-tuple-element.740) | copy-start | bytes 28 | tf_op jit(solution)/shard_map/while
  356.0 9.8 %copy-start.2 = (f32[3,48,128]{2,0,1:T(4,128)}, f32[3,48,128]{2,0,1:T(4,128)S(1)}, u32[]{:S(2)}) copy-start(f32[3,48,128]{2,0,1:T(4,128)S(1)} %get-tuple-element.745) | copy-start | bytes 221188 | tf_op jit(solution)/shard_map/while
  380.7 7.2 %copy-start.19 = (f32[1,2,1,1]{1,3,2,0:T(1,128)}, f32[1,2,1,1]{1,3,2,0:T(1,128)S(1)}, u32[]{:S(2)}) copy-start(f32[1,2,1,1]{1,3,2,0:T(1,128)S(1)} %get-tuple-element.740) | copy-start | bytes 28 | tf_op jit(solution)/shard_map/while
  380.8 9.8 %copy-start.2 = (f32[3,48,128]{2,0,1:T(4,128)}, f32[3,48,128]{2,0,1:T(4,128)S(1)}, u32[]{:S(2)}) copy-start(f32[3,48,128]{2,0,1:T(4,128)S(1)} %get-tuple-element.745) | copy-start | bytes 221188 | tf_op jit(solution)/shard_map/while
  405.5 7.2 %copy-start.19 = (f32[1,2,1,1]{1,3,2,0:T(1,128)}, f32[1,2,1,1]{1,3,2,0:T(1,128)S(1)}, u32[]{:S(2)}) copy-start(f32[1,2,1,1]{1,3,2,0:T(1,128)S(1)} %get-tuple-element.740) | copy-start | bytes 28 | tf_op jit(solution)/shard_map/while
  405.5 9.8 %copy-start.2 = (f32[3,48,128]{2,0,1:T(4,128)}, f32[3,48,128]{2,0,1:T(4,128)S(1)}, u32[]{:S(2)}) copy-start(f32[3,48,128]{2,0,1:T(4,128)S(1)} %get-tuple-element.745) | copy-start | bytes 221188 | tf_op jit(solution)/shard_map/while
  (133 other events, 458.1 us)
where the time goes:
time: 437 us; the launch traced here: 433 us
  other arithmetic  155 us (35%)
  blocking collectives  139 us (32%)
  local copies, waits for them, and re-layouts  73 us (17%)
  starting transfers between devices  42 us (10%)
  between operations  17.9 us (4%)
    unnamed x1, blocking collectives  62.1 us
    reduce_sum x27, other arithmetic, kernel_sum(): return jnp.sum(kernel * values[:, None, :], axis=2)  52.8 us
    sqrt x24, other arithmetic, kernel_sum(): distance = jnp.sqrt(squared + soften)  52 us
    psum x1, blocking collectives, body(): density = lax.psum(partial_value, 'orb')  30.8 us
    ppermute x5, starting transfers between devices, padded(): lax.ppermute(tail, axis, [(i, (i + 1) % count) for i in range(ends)])  28.6 us
    all_gather x1, blocking collectives, body(): lax.all_gather(source_plane, 'space', axis=1, tiled=True)  27.2 us
    all_gather x1, blocking collectives, body(): hartree = lax.all_gather(partial_field, 'orb', axis=0, tiled=True)  19 us
    gather x9, local copies, waits for them, and re-layouts, per_cell(): rim_values[:, near_slot, :] * near_live[None, :, None]  17.9 us
  transfers between devices with their start and end apart: 10, of which 0 were waited for; matrix products, arithmetic and copies ran while one was open for 4% of the time, Pallas kernels for 0%

commit v1 on v0

v1 whole, which is shorter than its diff:
```python
import functools
import math

import jax
import jax.numpy as jnp
from jax import lax
from jax.experimental import pallas as pl
from jax.experimental.pallas import tpu as pltpu
from jax.sharding import PartitionSpec as P

F32 = jnp.float32
BF16 = jnp.bfloat16
HI = lax.Precision.HIGHEST
LANES = (((1,), (1,)), ((), ()))
SOFTEN = 6.25e-06
SCALE = -0.5 / math.pi
SIDE = 0.25
NODE = [math.cos((2 * a + 1) * math.pi / 8) for a in range(4)]
OFFSET = [0.5 * (t + 1.0) for t in NODE]
FAR = 12
PLANE = 8
DENSE = FAR + PLANE
NEAR = 4 * 6 + 8 * 9 + 4 * 14


def iota(shape, axis):
    return lax.broadcasted_iota(jnp.int32, shape, axis)


def pick(index, table):
    out = jnp.full(index.shape, table[0], F32)
    for i in range(1, 4):
        out = jnp.where(index == i, F32(table[i]), out)
    return out


def pick_scalar(index, table):
    out = F32(table[0])
    for i in range(1, 4):
        out = jnp.where(index == i, F32(table[i]), out)
    return out


def select_rows(row, parts):
    out = jnp.where(row == 0, parts[0], parts[1])
    for i in range(2, 4):
        out = jnp.where(row == i, parts[i], out)
    return out


def lagrange(u):
    out = []
    for a in range(4):
        term = None
        for n in range(4):
            if n != a:
                factor = (u - NODE[n]) * (1.0 / (NODE[a] - NODE[n]))
                term = factor if term is None else term * factor
        out.append(term)
    return out


def near_count(t):
    cx, cy = t % 4, t // 4
    nx = jnp.where((cx == 0) | (cx == 3), 2, 3)
    ny = jnp.where((cy == 0) | (cy == 3), 2, 3)
    return 3 * nx * ny


def hi_lo(row):
    r = iota((16, row.shape[1]), 0)
    rest = row - row.astype(BF16).astype(F32)
    return jnp.where(r == 0, row, jnp.where(r == 1, rest, 0.0)).astype(BF16)


def kernel(
    orb, pts, qw, ext, screening, level, near, out, hart,
    G, TB, DXY, PR, CV, SV, MC, MS, LG, LP, A, AP, D0, D1, RA, RB,
    ZCO, ZCR, ZSO, ZSR, ZF, HG, FM, VN, VF, VP, send, recv,
):
    o = lax.axis_index("orb")
    g = lax.axis_index("space")
    core, x, y = g % 2, g // 2 % 4, g // 8
    zi, zb = o % 4, o // 4
    up, down = (g + 1) % 32, (g + 31) % 32
    lane = iota((1, 128), 1)

    def other_z(d):
        return {"orb": (o + d) % 16}

    def other_x(d):
        return {"space": g + 2 * ((x + d) % 4 - x)}

    def other_y(d):
        return {"space": g + 8 * ((y + d) % 4 - y)}

    barrier = pltpu.get_barrier_semaphore()
    partners = [other_z(d) for d in range(1, 16)]
    partners += [other_x(d) for d in range(1, 4)] + [other_y(d) for d in range(1, 4)]
    partners += [{"space": up}, {"space": down}]
    for partner in partners:
        pl.semaphore_signal(barrier, inc=1, device_id=partner, device_id_type=pl.DeviceIdType.MESH)

    def copy(src, dst, i, device, j=None):
        return pltpu.make_async_remote_copy(
            src, dst, send.at[i], recv.at[i if j is None else j],
            device_id=device, device_id_type=pl.DeviceIdType.MESH,
        )

    def rim(ref, i):
        return [
            copy(ref.at[1], ref.at[0], i, {"space": up}),
            copy(ref.at[1], ref.at[2], i + 1, {"space": down}),
        ]

    def begin(copies):
        for c in copies:
            c.start()

    def finish(copies):
        for c in copies:
            c.wait()

    rates = [-screening[level[v]] * (1.0 / math.log(2.0)) for v in range(2)]

    def columns(t):
        for k in range(3):
            TB[k] = jnp.broadcast_to(pts[k, pl.ds(t, 1), :], (128, 128)).T

    def green(r2):
        inv = lax.rsqrt(r2)
        s = r2 * inv
        return [(jnp.exp2(s * rate) * inv).astype(BF16) for rate in rates]

    def far_xy():
        a, b, c8 = lane // 4 % 4, lane % 4, lane // 16
        gx = (c8 % 4).astype(F32) * SIDE + SIDE * pick(a, OFFSET)
        dx = TB[0] - gx
        for half in range(2):
            gy = (c8 // 4 + 2 * half).astype(F32) * SIDE + SIDE * pick(b, OFFSET)
            dy = TB[1] - gy
            DXY[half] = dx * dx + (dy * dy + SOFTEN)

    def plane_z():
        gz = (lane // 4).astype(F32) * SIDE + SIDE * pick(lane % 4, OFFSET)
        dz = TB[2] - gz
        DXY[0] = dz * dz + SOFTEN

    def far_dz2(k):
        dz = TB[2] - ((g - 1 + k // 4).astype(F32) * SIDE + SIDE * pick_scalar(k % 4, OFFSET))
        return dz * dz

    def plane_xy2(ab):
        dx = TB[0] - pick_scalar(ab // 4, OFFSET)
        dy = TB[1] - pick_scalar(ab % 4, OFFSET)
        return dx * dx + dy * dy

    def store_green(block, half, r2):
        for v, values in enumerate(green(r2)):
            G[block, v, :, half * 128 : half * 128 + 128] = values

    def dense(lo, hi):
        def cell(t, carry):
            columns(t)
            far_xy()

            def far(k, c):
                dz2 = far_dz2(k)
                for half in range(2):
                    store_green(t * DENSE + k, half, DXY[half] + dz2)
                return c

            lax.fori_loop(0, FAR, far, 0)
            plane_z()

            def planes(k, c):
                for half in range(2):
                    store_green(t * DENSE + FAR + k, half, plane_xy2(2 * k + half) + DXY[0])
                return c

            lax.fori_loop(0, PLANE, planes, 0)
            return carry

        lax.fori_loop(lo, hi, cell, 0)

    def near_slot(t, n):
        cell = near[t, jnp.minimum(n, 26)]
        slot = jnp.clip(cell - 16 * (g - 1), 0, 47)
        return jnp.where((cell >= 0) & (n < 27), slot, 48)

    def near_r2(slot):
        lev, c = slot // 16, slot % 16
        total = None
        for k in range(3):
            d = TB[k] - PR[lev, k, pl.ds(c, 1), :]
            total = d * d + SOFTEN if total is None else total + d * d
        return total

    def near_green(lo, hi, off):
        def cell(t, off):
            columns(t)
            count = (near_count(t) + 1) // 2

            def pair(p, c):
                for half in range(2):
                    store_green(
                        DENSE * 16 + off + p, half, near_r2(near_slot(t, 2 * p + half))
                    )
                return c

            lax.fori_loop(0, count, pair, 0)
            return off + count

        return lax.fori_loop(lo, hi, cell, off)

    D0[...] = 2.0 * (orb[0] * orb[0] + orb[1] * orb[1])
    PR[1] = pts[...]
    PR[3] = jnp.zeros((3, 16, 128), F32)
    CV[3] = jnp.zeros((16, 128), F32)
    row16 = iota((16, 128), 0)
    ux = (pts[0] - (row16 % 4).astype(F32) * SIDE) * (2.0 / SIDE) - 1.0
    uy = (pts[1] - (row16 // 4).astype(F32) * SIDE) * (2.0 / SIDE) - 1.0
    uz = (pts[2] - g.astype(F32) * SIDE) * (2.0 / SIDE) - 1.0
    for k, u in enumerate((ux, uy, uz)):
        for a, w in enumerate(lagrange(u)):
            LG[k, a] = w
    for k in range(2):
        for a, w in enumerate(lagrange(2.0 * pts[k] - 1.0)):
            LP[k, a] = w
    row8 = iota((8, 128), 0)
    for c in range(16):
        one = slice(c, c + 1)
        ycell = select_rows(row8 % 4, [LG[1, b, one, :] for b in range(4)])
        yplane = select_rows(row8 % 4, [LP[1, b, one, :] for b in range(4)])
        for k in range(2):
            xcell = jnp.where(row8 < 4, LG[0, 2 * k, one, :], LG[0, 2 * k + 1, one, :])
            xplane = jnp.where(row8 < 4, LP[0, 2 * k, one, :], LP[0, 2 * k + 1, one, :])
            at = c % 8 * 16 + k * 8
            A[c // 8, at : at + 8, :] = xcell * ycell
            AP[k * 8 : k * 8 + 8, c * 128 : c * 128 + 128] = xplane * yplane

    def masks(t, carry):
        lev = g - 1 + row8 // 2
        cell = lev * 16 + row8 % 2 * 8 + lane // 16
        hit = (lev < 0) | (lev > 31)
        for n in range(27):
            hit = hit | (cell == near[t, n])
        FM[t] = jnp.where(hit, 0.0, 1.0)
        return carry

    lax.fori_loop(0, 16, masks, 0)
    dense(0, 4)
    pl.semaphore_wait(barrier, len(partners))

    first = [copy(D0, RA.at[d - 1], d - 1, {"orb": zb * 4 + (zi + d) % 4}) for d in range(1, 4)]
    begin(first)
    edge_points = rim(PR, 6)
    begin(edge_points)
    dense(4, 7)
    finish(first)
    D1[...] = D0[...] + (RA[0] + RA[1]) + RA[2]
    second = [
        copy(D1, RB.at[d - 1], 2 + d, {"orb": (zb + d) % 4 * 4 + zi}) for d in range(1, 4)
    ]
    begin(second)
    dense(7, 12)
    finish(second)
    weight = qw[...] * (SIDE**3 / 128)
    CV[1] = weight * (D1[...] + (RB[0] + RB[1]) + RB[2])

    def moments(values, cells):
        tiles = []
        for c in range(16):
            one = slice(c, c + 1)
            z = select_rows(row8 % 4, [LG[2, d, one, :] for d in range(4)])
            parts = [v[one, :] for v in values]
            tiles.append(z * jnp.where(row8 < 4, parts[0], parts[1] if len(parts) > 1 else 0.0))
        for half in range(2):
            rows = jnp.concatenate(tiles[half * 8 : half * 8 + 8], axis=0)
            every = lax.dot_general(rows, A[half], LANES, precision=HI, preferred_element_type=F32)
            total = jnp.zeros((8, 128), F32)
            for c in range(8):
                total = jnp.where(lane // 16 == c, every[c * 8 : c * 8 + 8], total)
            cells[1, half] = total
        wide = jnp.concatenate(tiles, axis=1)
        small = lax.dot_general(AP[...], wide, LANES, precision=HI, preferred_element_type=F32)
        planes = []
        for v in range(len(values)):
            spread = (iota((8, 128), 0) == v * 4 + lane % 4).astype(F32)
            planes.append(jnp.dot(small, spread, precision=HI, preferred_element_type=F32))
        return planes

    def gather_planes(planes, own, got, base, fill):
        for v, plane in enumerate(planes):
            own[0, v] = plane
        stage = [copy(own.at[0], got.at[0], base, {"space": g + 1 - 2 * core})]
        begin(stage)
        fill[0]()
        finish(stage)
        own[1] = jnp.where(lane // 4 % 2 == core, own[0], got[0])
        stage = [copy(own.at[1], got.at[d], base + d, other_x(d)) for d in range(1, 4)]
        begin(stage)
        fill[1]()
        finish(stage)
        full = own[1]
        for d in range(1, 4):
            full = jnp.where(lane // 8 % 4 == (x + 4 - d) % 4, got[d], full)
        own[2] = full
        stage = [copy(own.at[2], got.at[3 + d], base + 3 + d, other_y(d)) for d in range(1, 4)]
        begin(stage)
        fill[2]()
        finish(stage)
        full = own[2]
        for d in range(1, 4):
            full = jnp.where(lane // 32 == (y + 4 - d) % 4, got[3 + d], full)
        return jnp.where(jnp.abs(lane // 4 - g) >= 2, full, 0.0)

    nothing = lambda: None
    edge_charge = rim(CV, 8)
    begin(edge_charge)
    planes = moments([CV.at[1]], MC)
    edge_moments = rim(MC, 10)
    begin(edge_moments)
    full = gather_planes(
        planes, ZCO, ZCR, 12, [nothing, lambda: dense(12, 14), lambda: dense(14, 16)]
    )
    ZF[...] = full[0]
    finish(edge_points)
    finish(edge_charge)
    finish(edge_moments)

    columns(o)
    acc = jnp.zeros((128, 128), F32)

    def near_hartree(p, acc):
        for half in range(2):
            slot = near_slot(o, 2 * p + half)
            acc = acc + lax.rsqrt(near_r2(slot)) * CV[slot // 16, pl.ds(slot % 16, 1), :]
        return acc

    acc = lax.fori_loop(0, (near_count(o) + 1) // 2, near_hartree, acc)
    far_xy()

    def far_hartree(k, acc):
        dz2 = far_dz2(k)
        for half in range(2):
            row = MC[k // 4, half, pl.ds(k % 4, 1), :] * FM[o, pl.ds(k // 4 * 2 + half, 1), :]
            acc = acc + lax.rsqrt(DXY[half] + dz2) * row
        return acc

    acc = lax.fori_loop(0, FAR, far_hartree, acc)
    plane_z()

    def plane_hartree(k, acc):
        for half in range(2):
            ab = 2 * k + half
            acc = acc + lax.rsqrt(plane_xy2(ab) + DXY[0]) * ZF[pl.ds(ab, 1), :]
        return acc

    acc = lax.fori_loop(0, PLANE, plane_hartree, acc)
    summed = lax.dot_general(
        jnp.ones((8, 128), F32), acc, LANES, precision=HI, preferred_element_type=F32
    )
    HG[o] = summed[0:1]
    shares = [copy(HG.at[o], HG.at[o], 18 + d, other_z(d), 19 + o) for d in range(1, 16)]
    begin(shares)
    off = near_green(0, 8, 0)
    for d in range(1, 16):
        shares[d - 1].wait_send()
        k = (o + 16 - d) % 16
        copy(HG.at[k], HG.at[k], 18 + d, other_z(d), 19 + k).wait_recv()
    for c in range(16):
        hart[c : c + 1, :] = HG[c]

    scaled = weight * (ext[...] + hart[...])
    for v in range(2):
        SV[1, v] = scaled * orb[v]
    edge_sources = rim(SV, 35)
    begin(edge_sources)
    planes = moments([SV.at[1, 0], SV.at[1, 1]], MS)
    edge_moments = rim(MS, 37)
    begin(edge_moments)
    cells = [off]

    def more(lo, hi):
        cells[0] = near_green(lo, hi, cells[0])

    full = gather_planes(
        planes, ZSO, ZSR, 39, [lambda: more(8, 10), lambda: more(10, 12), lambda: more(12, 16)]
    )
    finish(edge_sources)
    finish(edge_moments)

    for v in range(2):
        VN[v, 48] = jnp.zeros((16, 128), BF16)
        for lev in range(3):
            for c in range(16):
                VN[v, lev * 16 + c] = hi_lo(SV[lev, v, c : c + 1, :])
            for d in range(4):
                for half in range(2):
                    r = v * 4 + d
                    VF[lev * 4 + d, v, :, half * 128 : half * 128 + 128] = hi_lo(
                        MS[lev, half, r : r + 1, :]
                    )
        for ab in range(16):
            half = ab % 2
            VP[ab // 2, v, :, half * 128 : half * 128 + 128] = hi_lo(full[v, ab : ab + 1, :])

    def product(rows, block, v):
        return lax.dot_general(rows, G[block, v], LANES, preferred_element_type=F32)

    def update(t, off):
        acc = [jnp.zeros((16, 128), F32) for _ in range(2)]
        for lev in range(3):
            mask = jnp.concatenate(
                [
                    jnp.broadcast_to(FM[t, lev * 2 + half : lev * 2 + half + 1, :], (16, 128))
                    for half in range(2)
                ],
                axis=1,
            ).astype(BF16)
            for d in range(4):
                k = lev * 4 + d
                for v in range(2):
                    acc[v] = acc[v] + product(VF[k, v] * mask, t * DENSE + k, v)
        for k in range(PLANE):
            for v in range(2):
                acc[v] = acc[v] + product(VP[k, v], t * DENSE + FAR + k, v)
        count = (near_count(t) + 1) // 2

        def pair(p, acc):
            s0, s1 = near_slot(t, 2 * p), near_slot(t, 2 * p + 1)
            return tuple(
                acc[v]
                + product(
                    jnp.concatenate([VN[v, s0], VN[v, s1]], axis=1), DENSE * 16 + off + p, v
                )
                for v in range(2)
            )

        acc = lax.fori_loop(0, count, pair, tuple(acc))
        for v in range(2):
            out[v, pl.ds(t, 1), :] = SCALE * (acc[v][0:1] + acc[v][1:2])
        return off + count

    lax.fori_loop(0, 16, update, 0)


def body(orbitals, points, quad_weight, external, screening, level_index, near_cells, far_cells):
    vmem = pl.BlockSpec(memory_space=pltpu.VMEM)
    smem = pl.BlockSpec(memory_space=pltpu.SMEM)

    def f32(*shape):
        return pltpu.VMEM(shape, F32)

    def bf16(*shape):
        return pltpu.VMEM(shape, BF16)

    return pl.pallas_call(
        kernel,
        out_shape=(
            jax.ShapeDtypeStruct((2, 16, 128), F32),
            jax.ShapeDtypeStruct((16, 128), F32),
        ),
        in_specs=[vmem] * 4 + [smem] * 3,
        out_specs=(vmem, vmem),
        scratch_shapes=[
            bf16(16 * DENSE + NEAR, 2, 128, 256),
            f32(3, 128, 128),
            f32(2, 128, 128),
            f32(4, 3, 16, 128),
            f32(4, 16, 128),
            f32(3, 2, 16, 128),
            f32(3, 2, 8, 128),
            f32(3, 2, 8, 128),
            f32(3, 4, 16, 128),
            f32(2, 4, 16, 128),
            f32(2, 128, 128),
            f32(16, 2048),
            f32(16, 128),
            f32(16, 128),
            f32(3, 16, 128),
            f32(3, 16, 128),
            f32(3, 1, 16, 128),
            f32(7, 1, 16, 128),
            f32(3, 2, 16, 128),
            f32(7, 2, 16, 128),
            f32(16, 128),
            f32(16, 1, 128),
            f32(16, 8, 128),
            bf16(2, 49, 16, 128),
            bf16(FAR, 2, 16, 256),
            bf16(PLANE, 2, 16, 256),
            pltpu.SemaphoreType.DMA((48,)),
            pltpu.SemaphoreType.DMA((48,)),
        ],
        compiler_params=pltpu.CompilerParams(
            collective_id=0, has_side_effects=True, vmem_limit_bytes=67043328
        ),
        name="green_step",
    )(orbitals, points, quad_weight, external, screening, level_index, near_cells)


def solution(mesh):
    in_specs = (
        P("orb", "space", None),
        P(None, "space", None),
        P("space", None),
        P("space", None),
        P(),
        P("orb"),
        P("space", None),
        P("space", None),
    )
    out_specs = (P("orb", "space", None), P("space", None))
    return jax.shard_map(body, mesh=mesh, in_specs=in_specs, out_specs=out_specs, check_vma=False)
```

time: 437 us -> 102 us (0.23)
  other arithmetic: 155 us -> 0 us
  blocking collectives: 139 us -> 0 us
  Pallas kernels: 0 us -> 99.6 us
  local copies, waits for them, and re-layouts: 73 us -> 1.93 us
  starting transfers between devices: 42 us -> 0 us
  between operations: 17.9 us -> 0.65 us
    pallas_call x0 -> x1, Pallas kernels: none -> 99.6 us  [body(): pl.pallas_call(kernel, out_shape=(jax.ShapeDtypeStruct((2, 16, 128), F32)...]
    unnamed x1 -> x0, blocking collectives: 62.1 us -> none
    gather x76 -> x0, local copies, waits for them, and re-layouts: 56 us -> none  [the longest x9 17.9 us: per_cell(): rim_values[:, near_slot, :] * near_live[None, :, None]]
    reduce_sum x29 -> x0, other arithmetic: 53.7 us -> none  [the longest x27 52.8 us: kernel_sum(): return jnp.sum(kernel * values[:, None, :], axis=2)]
    sqrt x24 -> x0, other arithmetic: 52 us -> none  [kernel_sum(): distance = jnp.sqrt(squared + soften)]
    all_gather x2 -> x0, blocking collectives: 46.2 us -> none  [the longest x1 27.2 us: body(): lax.all_gather(source_plane, 'space', axis=1, tiled=True)]
    ppermute x10 -> x0, starting transfers between devices: 42 us -> none  [the longest x5 28.6 us: padded(): lax.ppermute(tail, axis, [(i, (i + 1) % count) for i in range(ends)])]
    psum x1 -> x0, blocking collectives: 30.8 us -> none  [body(): density = lax.psum(partial_value, 'orb')]
  transfers between devices with their start and end apart: 10 -> 0, of which waited for: 0 -> 0; matrix products, arithmetic and copies ran while one was open for 4% -> 0% of each run, Pallas kernels for 0% -> 0%
where the time goes in v1:
time: 102 us
  Pallas kernels  99.6 us (98%)
  local copies, waits for them, and re-layouts  1.93 us (2%)
    pallas_call x1, Pallas kernels, body(): pl.pallas_call(kernel, out_shape=(jax.ShapeDtypeStruct((2, 16, 128), F32)...  99.6 us

profile of v1, /device:TPU:1, one launch (start us, length us, event | category | flops | bytes accessed | tf_op | source)
XLA Modules:
  0.0 102.1 jit_solution(11874242829368248659)
XLA Ops:
  0.6 99.6 %green_step.1 = (f32[2,16,128]{2,1,0:T(8,128)}, f32[16,128]{1,0:T(8,128)}) custom-call(f32[2,16,128]{2,1,0:T(8,128)} %orb.1, f32[3,16,128]{2,1,0:T(8,128)} %pts.1, f32[16,128]{1,0:T(8,128)} %qw.1, f32[16,128]{1,0:T(8,128)} %ext.1, f32[32]{0:T(128)} %screening.1, s32[2]{0:T(128)} %level.1, s32[16,27]{1,0:T(8,128)} %near.1), custom_call_target="tpu_custom_call" | custom-call | tf_op jit(solution)/shard_map/green_step/pallas_call | solution.py:459
  100.2 0.0 copy-start
  100.2 1.3 %copy.11 = f32[2,16,128]{2,1,0:T(8,128)} copy(f32[2,16,128]{2,1,0:T(8,128)} %get-tuple-element.4) | data formatting | bytes 32768
  101.5 0.0 copy-done
  101.5 0.6 copy.12
Async XLA Ops:
  100.2 1.3 %copy-start = (f32[16,128]{1,0:T(8,128)S(1)}, f32[16,128]{1,0:T(8,128)}, u32[]{:S(2)}) copy-start(f32[16,128]{1,0:T(8,128)} %get-tuple-element.5) | copy-start | bytes 24580

commit v2 on v1

--- a/solution.py
+++ b/solution.py
@@ -20,7 +20,7 @@
 FAR = 12
 PLANE = 8
 DENSE = FAR + PLANE
-NEAR = 4 * 6 + 8 * 9 + 4 * 14
+NEAR = 4 * 4 + 8 * 6 + 4 * 9
 
 
 def iota(shape, axis):
@@ -67,16 +67,10 @@
     return 3 * nx * ny
 
 
-def hi_lo(row):
-    r = iota((16, row.shape[1]), 0)
-    rest = row - row.astype(BF16).astype(F32)
-    return jnp.where(r == 0, row, jnp.where(r == 1, rest, 0.0)).astype(BF16)
-
-
 def kernel(
     orb, pts, qw, ext, screening, level, near, out, hart,
-    G, TB, DXY, PR, CV, SV, MC, MS, LG, LP, A, AP, D0, D1, RA, RB,
-    ZCO, ZCR, ZSO, ZSR, ZF, HG, FM, VN, VF, VP, send, recv,
+    G, GN, ACC, TB, DXY, PR, CV, SV, MC, MS, LG, LP, A, AP, D0, D1, RA, RB,
+    ZCO, ZCR, ZSO, ZSR, ZF, HG, FM, send, recv,
 ):
     o = lax.axis_index("orb")
     g = lax.axis_index("space")
@@ -164,29 +158,30 @@
             columns(t)
             far_xy()
 
-            def far(k, c):
-                dz2 = far_dz2(k)
-                for half in range(2):
-                    store_green(t * DENSE + k, half, DXY[half] + dz2)
+            def far(j, c):
+                for k in (2 * j, 2 * j + 1):
+                    dz2 = far_dz2(k)
+                    for half in range(2):
+                        store_green(t * DENSE + k, half, DXY[half] + dz2)
                 return c
 
-            lax.fori_loop(0, FAR, far, 0)
+            lax.fori_loop(0, FAR // 2, far, 0)
             plane_z()
 
-            def planes(k, c):
-                for half in range(2):
-                    store_green(t * DENSE + FAR + k, half, plane_xy2(2 * k + half) + DXY[0])
+            def planes(j, c):
+                for k in (2 * j, 2 * j + 1):
+                    for half in range(2):
+                        store_green(t * DENSE + FAR + k, half, plane_xy2(2 * k + half) + DXY[0])
                 return c
 
-            lax.fori_loop(0, PLANE, planes, 0)
+            lax.fori_loop(0, PLANE // 2, planes, 0)
             return carry
 
         lax.fori_loop(lo, hi, cell, 0)
 
     def near_slot(t, n):
-        cell = near[t, jnp.minimum(n, 26)]
-        slot = jnp.clip(cell - 16 * (g - 1), 0, 47)
-        return jnp.where((cell >= 0) & (n < 27), slot, 48)
+        cell = near[t, n]
+        return jnp.where(cell >= 0, jnp.clip(cell - 16 * (g - 1), 0, 47), 48)
 
     def near_r2(slot):
         lev, c = slot // 16, slot % 16
@@ -199,16 +194,15 @@
     def near_green(lo, hi, off):
         def cell(t, off):
             columns(t)
-            count = (near_count(t) + 1) // 2
-
-            def pair(p, c):
-                for half in range(2):
-                    store_green(
-                        DENSE * 16 + off + p, half, near_r2(near_slot(t, 2 * p + half))
-                    )
+            count = near_count(t) // 3
+
+            def triple(p, c):
+                for i in range(3):
+                    for v, values in enumerate(green(near_r2(near_slot(t, 3 * p + i)))):
+                        GN[off + p, v, i] = values
                 return c
 
-            lax.fori_loop(0, count, pair, 0)
+            lax.fori_loop(0, count, triple, 0)
             return off + count
 
         return lax.fori_loop(lo, hi, cell, off)
@@ -217,6 +211,7 @@
     PR[1] = pts[...]
     PR[3] = jnp.zeros((3, 16, 128), F32)
     CV[3] = jnp.zeros((16, 128), F32)
+    SV[3] = jnp.zeros((2, 16, 128), F32)
     row16 = iota((16, 128), 0)
     ux = (pts[0] - (row16 % 4).astype(F32) * SIDE) * (2.0 / SIDE) - 1.0
     uy = (pts[1] - (row16 // 4).astype(F32) * SIDE) * (2.0 / SIDE) - 1.0
@@ -249,21 +244,21 @@
         return carry
 
     lax.fori_loop(0, 16, masks, 0)
-    dense(0, 4)
+    dense(0, 5)
     pl.semaphore_wait(barrier, len(partners))
 
     first = [copy(D0, RA.at[d - 1], d - 1, {"orb": zb * 4 + (zi + d) % 4}) for d in range(1, 4)]
     begin(first)
     edge_points = rim(PR, 6)
     begin(edge_points)
-    dense(4, 7)
+    dense(5, 8)
     finish(first)
     D1[...] = D0[...] + (RA[0] + RA[1]) + RA[2]
     second = [
         copy(D1, RB.at[d - 1], 2 + d, {"orb": (zb + d) % 4 * 4 + zi}) for d in range(1, 4)
     ]
     begin(second)
-    dense(7, 12)
+    dense(8, 14)
     finish(second)
     weight = qw[...] * (SIDE**3 / 128)
     CV[1] = weight * (D1[...] + (RB[0] + RB[1]) + RB[2])
@@ -315,17 +310,22 @@
             full = jnp.where(lane // 32 == (y + 4 - d) % 4, got[3 + d], full)
         return jnp.where(jnp.abs(lane // 4 - g) >= 2, full, 0.0)
 
-    nothing = lambda: None
+    offset = [0]
+
+    def more(lo, hi):
+        offset[0] = near_green(lo, hi, offset[0])
+
     edge_charge = rim(CV, 8)
     begin(edge_charge)
     planes = moments([CV.at[1]], MC)
     edge_moments = rim(MC, 10)
     begin(edge_moments)
+    finish(edge_points)
     full = gather_planes(
-        planes, ZCO, ZCR, 12, [nothing, lambda: dense(12, 14), lambda: dense(14, 16)]
+        planes, ZCO, ZCR, 12, [lambda: more(0, 2), lambda: dense(14, 16), lambda: more(2, 6)]
     )
-    ZF[...] = full[0]
-    finish(edge_points)
+    for v in range(1):
+        ZF[v] = full[v]
     finish(edge_charge)
     finish(edge_moments)
 
@@ -333,12 +333,12 @@
     acc = jnp.zeros((128, 128), F32)
 
     def near_hartree(p, acc):
-        for half in range(2):
-            slot = near_slot(o, 2 * p + half)
+        for i in range(3):
+            slot = near_slot(o, 3 * p + i)
             acc = acc + lax.rsqrt(near_r2(slot)) * CV[slot // 16, pl.ds(slot % 16, 1), :]
         return acc
 
-    acc = lax.fori_loop(0, (near_count(o) + 1) // 2, near_hartree, acc)
+    acc = lax.fori_loop(0, near_count(o) // 3, near_hartree, acc)
     far_xy()
 
     def far_hartree(k, acc):
@@ -354,17 +354,14 @@
     def plane_hartree(k, acc):
         for half in range(2):
             ab = 2 * k + half
-            acc = acc + lax.rsqrt(plane_xy2(ab) + DXY[0]) * ZF[pl.ds(ab, 1), :]
+            acc = acc + lax.rsqrt(plane_xy2(ab) + DXY[0]) * ZF[0, pl.ds(ab, 1), :]
         return acc
 
     acc = lax.fori_loop(0, PLANE, plane_hartree, acc)
-    summed = lax.dot_general(
-        jnp.ones((8, 128), F32), acc, LANES, precision=HI, preferred_element_type=F32
-    )
-    HG[o] = summed[0:1]
+    HG[o] = jnp.sum(acc.T, axis=0, keepdims=True)
     shares = [copy(HG.at[o], HG.at[o], 18 + d, other_z(d), 19 + o) for d in range(1, 16)]
     begin(shares)
-    off = near_green(0, 8, 0)
+    more(6, 16)
     for d in range(1, 16):
         shares[d - 1].wait_send()
         k = (o + 16 - d) % 16
@@ -380,68 +377,67 @@
     planes = moments([SV.at[1, 0], SV.at[1, 1]], MS)
     edge_moments = rim(MS, 37)
     begin(edge_moments)
-    cells = [off]
-
-    def more(lo, hi):
-        cells[0] = near_green(lo, hi, cells[0])
+
+    def local(lo, hi, off):
+        def cell(t, off):
+            def far(lev, acc):
+                acc = list(acc)
+                for half in range(2):
+                    mask = FM[t, pl.ds(lev * 2 + half, 1), :]
+                    for d in range(4):
+                        for v in range(2):
+                            r = v * 4 + d
+                            row = MS[lev, half, r : r + 1, :] * mask
+                            values = G[t * DENSE + lev * 4 + d, v, :, half * 128 : half * 128 + 128]
+                            acc[v] = acc[v] + values.astype(F32) * row
+                return tuple(acc)
+
+            acc = lax.fori_loop(0, 3, far, (jnp.zeros((128, 128), F32),) * 2)
+            count = near_count(t) // 3
+
+            def triple(p, acc):
+                acc = list(acc)
+                for i in range(3):
+                    slot = near_slot(t, 3 * p + i)
+                    for v in range(2):
+                        row = SV[slot // 16, v, pl.ds(slot % 16, 1), :]
+                        acc[v] = acc[v] + GN[off + p, v, i].astype(F32) * row
+                return tuple(acc)
+
+            acc = lax.fori_loop(0, count, triple, acc)
+            for v in range(2):
+                ACC[t, v] = acc[v]
+            return off + count
+
+        return lax.fori_loop(lo, hi, cell, off)
+
+    done = [0]
+
+    def apply(lo, hi):
+        done[0] = local(lo, hi, done[0])
+
+    def arrived():
+        finish(edge_sources)
+        finish(edge_moments)
+        apply(0, 5)
 
     full = gather_planes(
-        planes, ZSO, ZSR, 39, [lambda: more(8, 10), lambda: more(10, 12), lambda: more(12, 16)]
+        planes, ZSO, ZSR, 39, [lambda: None, arrived, lambda: apply(5, 11)]
     )
-    finish(edge_sources)
-    finish(edge_moments)
-
     for v in range(2):
-        VN[v, 48] = jnp.zeros((16, 128), BF16)
-        for lev in range(3):
-            for c in range(16):
-                VN[v, lev * 16 + c] = hi_lo(SV[lev, v, c : c + 1, :])
-            for d in range(4):
+        ZF[v] = full[v]
+    apply(11, 16)
+
+    def update(t, carry):
+        for v in range(2):
+            acc = ACC[t, v]
+            for k in range(PLANE):
                 for half in range(2):
-                    r = v * 4 + d
-                    VF[lev * 4 + d, v, :, half * 128 : half * 128 + 128] = hi_lo(
-                        MS[lev, half, r : r + 1, :]
-                    )
-        for ab in range(16):
-            half = ab % 2
-            VP[ab // 2, v, :, half * 128 : half * 128 + 128] = hi_lo(full[v, ab : ab + 1, :])
-
-    def product(rows, block, v):
-        return lax.dot_general(rows, G[block, v], LANES, preferred_element_type=F32)
-
-    def update(t, off):
-        acc = [jnp.zeros((16, 128), F32) for _ in range(2)]
-        for lev in range(3):
-            mask = jnp.concatenate(
-                [
-                    jnp.broadcast_to(FM[t, lev * 2 + half : lev * 2 + half + 1, :], (16, 128))
-                    for half in range(2)
-                ],
-                axis=1,
-            ).astype(BF16)
-            for d in range(4):
-                k = lev * 4 + d
-                for v in range(2):
-                    acc[v] = acc[v] + product(VF[k, v] * mask, t * DENSE + k, v)
-        for k in range(PLANE):
-            for v in range(2):
-                acc[v] = acc[v] + product(VP[k, v], t * DENSE + FAR + k, v)
-        count = (near_count(t) + 1) // 2
-
-        def pair(p, acc):
-            s0, s1 = near_slot(t, 2 * p), near_slot(t, 2 * p + 1)
-            return tuple(
-                acc[v]
-                + product(
-                    jnp.concatenate([VN[v, s0], VN[v, s1]], axis=1), DENSE * 16 + off + p, v
-                )
-                for v in range(2)
-            )
-
-        acc = lax.fori_loop(0, count, pair, tuple(acc))
-        for v in range(2):
-            out[v, pl.ds(t, 1), :] = SCALE * (acc[v][0:1] + acc[v][1:2])
-        return off + count
+                    ab = 2 * k + half
+                    values = G[t * DENSE + FAR + k, v, :, half * 128 : half * 128 + 128]
+                    acc = acc + values.astype(F32) * ZF[v, ab : ab + 1, :]
+            out[v, pl.ds(t, 1), :] = SCALE * jnp.sum(acc.T, axis=0, keepdims=True)
+        return carry
 
     lax.fori_loop(0, 16, update, 0)
 
@@ -465,12 +461,14 @@
         in_specs=[vmem] * 4 + [smem] * 3,
         out_specs=(vmem, vmem),
         scratch_shapes=[
-            bf16(16 * DENSE + NEAR, 2, 128, 256),
+            bf16(16 * DENSE, 2, 128, 256),
+            bf16(NEAR, 2, 3, 128, 128),
+            f32(16, 2, 128, 128),
             f32(3, 128, 128),
             f32(2, 128, 128),
             f32(4, 3, 16, 128),
             f32(4, 16, 128),
-            f32(3, 2, 16, 128),
+            f32(4, 2, 16, 128),
             f32(3, 2, 8, 128),
             f32(3, 2, 8, 128),
             f32(3, 4, 16, 128),
@@ -485,12 +483,9 @@
             f32(7, 1, 16, 128),
             f32(3, 2, 16, 128),
             f32(7, 2, 16, 128),
-            f32(16, 128),
+            f32(2, 16, 128),
             f32(16, 1, 128),
             f32(16, 8, 128),
-            bf16(2, 49, 16, 128),
-            bf16(FAR, 2, 16, 256),
-            bf16(PLANE, 2, 16, 256),
             pltpu.SemaphoreType.DMA((48,)),
             pltpu.SemaphoreType.DMA((48,)),
         ],

time: 102 us -> 78.9 us (0.77)
  Pallas kernels: 99.6 us -> 76 us
    pallas_call x1, Pallas kernels: 99.6 us -> 76 us  [body(): pl.pallas_call(kernel, out_shape=(jax.ShapeDtypeStruct((2, 16, 128), F32)...]
where the time goes in v2:
time: 78.9 us; the launch traced here: 78.6 us
  Pallas kernels  76 us (96%)
  local copies, waits for them, and re-layouts  1.93 us (2%)
    pallas_call x1, Pallas kernels, body(): pl.pallas_call(kernel, out_shape=(jax.ShapeDtypeStruct((2, 16, 128), F32)...  76 us
    unnamed x4, local copies, waits for them, and re-layouts  1.93 us

profile of v2, /device:TPU:1, one launch (start us, length us, event | category | flops | bytes accessed | tf_op | source)
XLA Modules:
  0.0 78.6 jit_solution(2817148184223531423)
XLA Ops:
  0.6 76.0 %green_step.1 = (f32[2,16,128]{2,1,0:T(8,128)}, f32[16,128]{1,0:T(8,128)}) custom-call(f32[2,16,128]{2,1,0:T(8,128)} %orb.1, f32[3,16,128]{2,1,0:T(8,128)} %pts.1, f32[16,128]{1,0:T(8,128)} %qw.1, f32[16,128]{1,0:T(8,128)} %ext.1, f32[32]{0:T(128)} %screening.1, s32[2]{0:T(128)} %level.1, s32[16,27]{1,0:T(8,128)} %near.1), custom_call_target="tpu_custom_call" | custom-call | tf_op jit(solution)/shard_map/green_step/pallas_call | solution.py:455
  76.7 0.0 copy-start
  76.7 1.3 %copy.11 = f32[2,16,128]{2,1,0:T(8,128)} copy(f32[2,16,128]{2,1,0:T(8,128)} %get-tuple-element.4) | data formatting | bytes 32768
  78.0 0.0 copy-done
  78.0 0.6 copy.12
Async XLA Ops:
  76.7 1.3 %copy-start = (f32[16,128]{1,0:T(8,128)S(1)}, f32[16,128]{1,0:T(8,128)}, u32[]{:S(2)}) copy-start(f32[16,128]{1,0:T(8,128)} %get-tuple-element.5) | copy-start | bytes 24580

commit v3 on v2

--- a/solution.py
+++ b/solution.py
@@ -17,8 +17,8 @@
 SIDE = 0.25
 NODE = [math.cos((2 * a + 1) * math.pi / 8) for a in range(4)]
 OFFSET = [0.5 * (t + 1.0) for t in NODE]
-FAR = 12
-PLANE = 8
+FAR = 24
+PLANE = 16
 DENSE = FAR + PLANE
 NEAR = 4 * 4 + 8 * 6 + 4 * 9
 
@@ -69,37 +69,38 @@
 
 def kernel(
     orb, pts, qw, ext, screening, level, near, out, hart,
-    G, GN, ACC, TB, DXY, PR, CV, SV, MC, MS, LG, LP, A, AP, D0, D1, RA, RB,
-    ZCO, ZCR, ZSO, ZSR, ZF, HG, FM, send, recv,
+    G, GN, ACC, TB, DXY, PR, CV, SV, MC, MS, LG, LP, A, AP, D0, RA,
+    QC, RC, QS, RS, ZF, HG, FM, send, recv,
 ):
     o = lax.axis_index("orb")
     g = lax.axis_index("space")
-    core, x, y = g % 2, g // 2 % 4, g // 8
-    zi, zb = o % 4, o // 4
     up, down = (g + 1) % 32, (g + 31) % 32
     lane = iota((1, 128), 1)
+    away = lane // 8 + 16 * (lane // 4 % 2)
+    level_of = (g + 32 - away) % 32
 
     def other_z(d):
         return {"orb": (o + d) % 16}
 
-    def other_x(d):
-        return {"space": g + 2 * ((x + d) % 4 - x)}
-
-    def other_y(d):
-        return {"space": g + 8 * ((y + d) % 4 - y)}
+    def other_g(d):
+        return {"space": (g + d) % 32}
 
     barrier = pltpu.get_barrier_semaphore()
     partners = [other_z(d) for d in range(1, 16)]
-    partners += [other_x(d) for d in range(1, 4)] + [other_y(d) for d in range(1, 4)]
-    partners += [{"space": up}, {"space": down}]
+    partners += [other_g(d) for d in range(1, 32)]
     for partner in partners:
         pl.semaphore_signal(barrier, inc=1, device_id=partner, device_id_type=pl.DeviceIdType.MESH)
 
-    def copy(src, dst, i, device, j=None):
+    def copy(src, dst, i, device):
         return pltpu.make_async_remote_copy(
-            src, dst, send.at[i], recv.at[i if j is None else j],
+            src, dst, send.at[i], recv.at[i],
             device_id=device, device_id_type=pl.DeviceIdType.MESH,
         )
+
+    def all_of(ref, i, device):
+        whole = copy(ref, ref, i, device)
+        whole.wait_send()
+        whole.wait_recv()
 
     def rim(ref, i):
         return [
@@ -136,45 +137,47 @@
             DXY[half] = dx * dx + (dy * dy + SOFTEN)
 
     def plane_z():
-        gz = (lane // 4).astype(F32) * SIDE + SIDE * pick(lane % 4, OFFSET)
+        gz = level_of.astype(F32) * SIDE + SIDE * pick(lane % 4, OFFSET)
         dz = TB[2] - gz
         DXY[0] = dz * dz + SOFTEN
-
-    def far_dz2(k):
-        dz = TB[2] - ((g - 1 + k // 4).astype(F32) * SIDE + SIDE * pick_scalar(k % 4, OFFSET))
+        for b in range(4):
+            dy = TB[1] - OFFSET[b]
+            DXY[1 + b] = dy * dy
+
+    def far_dz2(lev, d):
+        dz = TB[2] - ((g - 1 + lev).astype(F32) * SIDE + SIDE * OFFSET[d])
         return dz * dz
 
-    def plane_xy2(ab):
-        dx = TB[0] - pick_scalar(ab // 4, OFFSET)
-        dy = TB[1] - pick_scalar(ab % 4, OFFSET)
-        return dx * dx + dy * dy
-
-    def store_green(block, half, r2):
+    def plane_xz2(a):
+        dx = TB[0] - pick_scalar(a, OFFSET)
+        return dx * dx + DXY[0]
+
+    def store_green(block, r2):
         for v, values in enumerate(green(r2)):
-            G[block, v, :, half * 128 : half * 128 + 128] = values
+            G[block, v] = values
 
     def dense(lo, hi):
         def cell(t, carry):
             columns(t)
             far_xy()
 
-            def far(j, c):
-                for k in (2 * j, 2 * j + 1):
-                    dz2 = far_dz2(k)
+            def far(lev, c):
+                for d in range(4):
+                    dz2 = far_dz2(lev, d)
                     for half in range(2):
-                        store_green(t * DENSE + k, half, DXY[half] + dz2)
+                        store_green(t * DENSE + lev * 8 + d * 2 + half, DXY[half] + dz2)
                 return c
 
-            lax.fori_loop(0, FAR // 2, far, 0)
+            lax.fori_loop(0, 3, far, 0)
             plane_z()
 
-            def planes(j, c):
-                for k in (2 * j, 2 * j + 1):
-                    for half in range(2):
-                        store_green(t * DENSE + FAR + k, half, plane_xy2(2 * k + half) + DXY[0])
+            def planes(a, c):
+                xz2 = plane_xz2(a)
+                for b in range(4):
+                    store_green(t * DENSE + FAR + a * 4 + b, xz2 + DXY[1 + b])
                 return c
 
-            lax.fori_loop(0, PLANE // 2, planes, 0)
+            lax.fori_loop(0, 4, planes, 0)
             return carry
 
         lax.fori_loop(lo, hi, cell, 0)
@@ -247,21 +250,17 @@
     dense(0, 5)
     pl.semaphore_wait(barrier, len(partners))
 
-    first = [copy(D0, RA.at[d - 1], d - 1, {"orb": zb * 4 + (zi + d) % 4}) for d in range(1, 4)]
-    begin(first)
-    edge_points = rim(PR, 6)
+    spread = [copy(D0, RA.at[d - 1], 0, other_z(d)) for d in range(1, 16)]
+    begin(spread)
+    edge_points = rim(PR, 1)
     begin(edge_points)
-    dense(5, 8)
-    finish(first)
-    D1[...] = D0[...] + (RA[0] + RA[1]) + RA[2]
-    second = [
-        copy(D1, RB.at[d - 1], 2 + d, {"orb": (zb + d) % 4 * 4 + zi}) for d in range(1, 4)
-    ]
-    begin(second)
-    dense(8, 14)
-    finish(second)
+    dense(5, 14)
+    all_of(RA, 0, other_z(1))
+    total = D0[...]
+    for d in range(15):
+        total = total + RA[d]
     weight = qw[...] * (SIDE**3 / 128)
-    CV[1] = weight * (D1[...] + (RB[0] + RB[1]) + RB[2])
+    CV[1] = weight * total
 
     def moments(values, cells):
         tiles = []
@@ -278,54 +277,39 @@
                 total = jnp.where(lane // 16 == c, every[c * 8 : c * 8 + 8], total)
             cells[1, half] = total
         wide = jnp.concatenate(tiles, axis=1)
-        small = lax.dot_general(AP[...], wide, LANES, precision=HI, preferred_element_type=F32)
-        planes = []
-        for v in range(len(values)):
-            spread = (iota((8, 128), 0) == v * 4 + lane % 4).astype(F32)
-            planes.append(jnp.dot(small, spread, precision=HI, preferred_element_type=F32))
-        return planes
-
-    def gather_planes(planes, own, got, base, fill):
-        for v, plane in enumerate(planes):
-            own[0, v] = plane
-        stage = [copy(own.at[0], got.at[0], base, {"space": g + 1 - 2 * core})]
-        begin(stage)
-        fill[0]()
-        finish(stage)
-        own[1] = jnp.where(lane // 4 % 2 == core, own[0], got[0])
-        stage = [copy(own.at[1], got.at[d], base + d, other_x(d)) for d in range(1, 4)]
-        begin(stage)
-        fill[1]()
-        finish(stage)
-        full = own[1]
-        for d in range(1, 4):
-            full = jnp.where(lane // 8 % 4 == (x + 4 - d) % 4, got[d], full)
-        own[2] = full
-        stage = [copy(own.at[2], got.at[3 + d], base + 3 + d, other_y(d)) for d in range(1, 4)]
-        begin(stage)
-        fill[2]()
-        finish(stage)
-        full = own[2]
-        for d in range(1, 4):
-            full = jnp.where(lane // 32 == (y + 4 - d) % 4, got[3 + d], full)
-        return jnp.where(jnp.abs(lane // 4 - g) >= 2, full, 0.0)
+        return lax.dot_general(wide, AP[...], LANES, precision=HI, preferred_element_type=F32)
+
+    def send_planes(small, own, got, i):
+        own[...] = jnp.zeros((8, 128), F32)
+        own[:, 0:16] = small
+        got[0] = own[...]
+        begin([copy(own, got.at[d], i, other_g(d)) for d in range(1, 32)])
+
+    def take_planes(got, i, count):
+        all_of(got.at[1:32], i, other_g(1))
+        low = got[0:16].reshape(128, 128).T[0:16]
+        high = got[16:32].reshape(128, 128).T[0:16]
+        first = lane // 4 % 2 == 0
+        parts = [jnp.where(first, low, pltpu.roll(high, 4, 1))]
+        if count == 2:
+            parts.append(jnp.where(first, pltpu.roll(low, 124, 1), high))
+        for v, part in enumerate(parts):
+            ZF[v] = jnp.where(jnp.abs(level_of - g) >= 2, part, 0.0)
 
     offset = [0]
 
     def more(lo, hi):
         offset[0] = near_green(lo, hi, offset[0])
 
-    edge_charge = rim(CV, 8)
+    edge_charge = rim(CV, 3)
     begin(edge_charge)
-    planes = moments([CV.at[1]], MC)
-    edge_moments = rim(MC, 10)
+    small = moments([CV.at[1]], MC)
+    edge_moments = rim(MC, 5)
     begin(edge_moments)
+    send_planes(small, QC, RC, 7)
+    dense(14, 16)
     finish(edge_points)
-    full = gather_planes(
-        planes, ZCO, ZCR, 12, [lambda: more(0, 2), lambda: dense(14, 16), lambda: more(2, 6)]
-    )
-    for v in range(1):
-        ZF[v] = full[v]
+    more(0, 1)
     finish(edge_charge)
     finish(edge_moments)
 
@@ -341,58 +325,68 @@
     acc = lax.fori_loop(0, near_count(o) // 3, near_hartree, acc)
     far_xy()
 
-    def far_hartree(k, acc):
-        dz2 = far_dz2(k)
+    def far_hartree(lev, acc):
         for half in range(2):
-            row = MC[k // 4, half, pl.ds(k % 4, 1), :] * FM[o, pl.ds(k // 4 * 2 + half, 1), :]
-            acc = acc + lax.rsqrt(DXY[half] + dz2) * row
+            mask = FM[o, pl.ds(lev * 2 + half, 1), :]
+            for d in range(4):
+                row = MC[lev, half, d : d + 1, :] * mask
+                acc = acc + lax.rsqrt(DXY[half] + far_dz2(lev, d)) * row
         return acc
 
-    acc = lax.fori_loop(0, FAR, far_hartree, acc)
+    acc = lax.fori_loop(0, 3, far_hartree, acc)
     plane_z()
-
-    def plane_hartree(k, acc):
-        for half in range(2):
-            ab = 2 * k + half
-            acc = acc + lax.rsqrt(plane_xy2(ab) + DXY[0]) * ZF[0, pl.ds(ab, 1), :]
+    take_planes(RC, 7, 1)
+
+    def plane_hartree(a, acc):
+        xz2 = plane_xz2(a)
+        for b in range(4):
+            acc = acc + lax.rsqrt(xz2 + DXY[1 + b]) * ZF[0, pl.ds(a * 4 + b, 1), :]
         return acc
 
-    acc = lax.fori_loop(0, PLANE, plane_hartree, acc)
-    HG[o] = jnp.sum(acc.T, axis=0, keepdims=True)
-    shares = [copy(HG.at[o], HG.at[o], 18 + d, other_z(d), 19 + o) for d in range(1, 16)]
-    begin(shares)
-    more(6, 16)
-    for d in range(1, 16):
-        shares[d - 1].wait_send()
-        k = (o + 16 - d) % 16
-        copy(HG.at[k], HG.at[k], 18 + d, other_z(d), 19 + k).wait_recv()
-    for c in range(16):
-        hart[c : c + 1, :] = HG[c]
+    acc = lax.fori_loop(0, 4, plane_hartree, acc)
+    HG[0] = jnp.sum(acc.T, axis=0, keepdims=True)
+    begin([copy(HG.at[0], HG.at[d], 8, other_z(d)) for d in range(1, 16)])
+    more(1, 11)
+    all_of(HG.at[1:16], 8, other_z(1))
+    for d in range(16):
+        hart[pl.ds((o + 16 - d) % 16, 1), :] = HG[d]
 
     scaled = weight * (ext[...] + hart[...])
     for v in range(2):
         SV[1, v] = scaled * orb[v]
-    edge_sources = rim(SV, 35)
+    edge_sources = rim(SV, 9)
     begin(edge_sources)
-    planes = moments([SV.at[1, 0], SV.at[1, 1]], MS)
-    edge_moments = rim(MS, 37)
+    small = moments([SV.at[1, 0], SV.at[1, 1]], MS)
+    edge_moments = rim(MS, 11)
     begin(edge_moments)
+    send_planes(small, QS, RS, 13)
+    more(11, 16)
+
+    def weigh(values, rows):
+        total = None
+        for value, row in zip(values, rows):
+            wide = jnp.broadcast_to(row, (16, 128)).astype(BF16)
+            term = value.reshape(8, 16, 128) * wide[None]
+            total = term if total is None else total + term
+        return total.astype(F32)
 
     def local(lo, hi, off):
         def cell(t, off):
             def far(lev, acc):
                 acc = list(acc)
-                for half in range(2):
-                    mask = FM[t, pl.ds(lev * 2 + half, 1), :]
-                    for d in range(4):
-                        for v in range(2):
-                            r = v * 4 + d
-                            row = MS[lev, half, r : r + 1, :] * mask
-                            values = G[t * DENSE + lev * 4 + d, v, :, half * 128 : half * 128 + 128]
-                            acc[v] = acc[v] + values.astype(F32) * row
+                masks = [FM[t, pl.ds(lev * 2 + half, 1), :] for half in range(2)]
+                for d in range(4):
+                    for v in range(2):
+                        r = v * 4 + d
+                        at = t * DENSE + lev * 8 + d * 2
+                        acc[v] = acc[v] + weigh(
+                            [G[at, v], G[at + 1, v]],
+                            [MS[lev, half, r : r + 1, :] * masks[half] for half in range(2)],
+                        )
                 return tuple(acc)
 
-            acc = lax.fori_loop(0, 3, far, (jnp.zeros((128, 128), F32),) * 2)
+            acc = lax.fori_loop(0, 3, far, (jnp.zeros((8, 16, 128), F32),) * 2)
+            acc = tuple(a.reshape(128, 128) for a in acc)
             count = near_count(t) // 3
 
             def triple(p, acc):
@@ -416,26 +410,21 @@
     def apply(lo, hi):
         done[0] = local(lo, hi, done[0])
 
-    def arrived():
-        finish(edge_sources)
-        finish(edge_moments)
-        apply(0, 5)
-
-    full = gather_planes(
-        planes, ZSO, ZSR, 39, [lambda: None, arrived, lambda: apply(5, 11)]
-    )
-    for v in range(2):
-        ZF[v] = full[v]
-    apply(11, 16)
+    finish(edge_sources)
+    finish(edge_moments)
+    apply(0, 16)
+    take_planes(RS, 13, 2)
 
     def update(t, carry):
         for v in range(2):
             acc = ACC[t, v]
-            for k in range(PLANE):
-                for half in range(2):
-                    ab = 2 * k + half
-                    values = G[t * DENSE + FAR + k, v, :, half * 128 : half * 128 + 128]
-                    acc = acc + values.astype(F32) * ZF[v, ab : ab + 1, :]
+            acc = acc.reshape(8, 16, 128)
+            for ab in range(0, PLANE, 2):
+                at = t * DENSE + FAR + ab
+                acc = acc + weigh(
+                    [G[at, v], G[at + 1, v]], [ZF[v, ab : ab + 1, :], ZF[v, ab + 1 : ab + 2, :]]
+                )
+            acc = acc.reshape(128, 128)
             out[v, pl.ds(t, 1), :] = SCALE * jnp.sum(acc.T, axis=0, keepdims=True)
         return carry
 
@@ -461,11 +450,11 @@
         in_specs=[vmem] * 4 + [smem] * 3,
         out_specs=(vmem, vmem),
         scratch_shapes=[
-            bf16(16 * DENSE, 2, 128, 256),
+            bf16(16 * DENSE, 2, 128, 128),
             bf16(NEAR, 2, 3, 128, 128),
             f32(16, 2, 128, 128),
             f32(3, 128, 128),
-            f32(2, 128, 128),
+            f32(5, 128, 128),
             f32(4, 3, 16, 128),
             f32(4, 16, 128),
             f32(4, 2, 16, 128),
@@ -476,18 +465,16 @@
             f32(2, 128, 128),
             f32(16, 2048),
             f32(16, 128),
-            f32(16, 128),
-            f32(3, 16, 128),
-            f32(3, 16, 128),
-            f32(3, 1, 16, 128),
-            f32(7, 1, 16, 128),
-            f32(3, 2, 16, 128),
-            f32(7, 2, 16, 128),
+            f32(15, 16, 128),
+            f32(8, 128),
+            f32(32, 8, 128),
+            f32(8, 128),
+            f32(32, 8, 128),
             f32(2, 16, 128),
             f32(16, 1, 128),
             f32(16, 8, 128),
-            pltpu.SemaphoreType.DMA((48,)),
-            pltpu.SemaphoreType.DMA((48,)),
+            pltpu.SemaphoreType.DMA((14,)),
+            pltpu.SemaphoreType.DMA((14,)),
         ],
         compiler_params=pltpu.CompilerParams(
             collective_id=0, has_side_effects=True, vmem_limit_bytes=67043328

time: 78.9 us -> 73.7 us (0.934)
  Pallas kernels: 76 us -> 70.9 us
    pallas_call x1, Pallas kernels: 76 us -> 70.9 us  [body(): pl.pallas_call(kernel, out_shape=(jax.ShapeDtypeStruct((2, 16, 128), F32)...]
where the time goes in v3:
time: 73.7 us; the launch traced here: 73.5 us
  Pallas kernels  70.9 us (96%)
  local copies, waits for them, and re-layouts  1.93 us (3%)
    pallas_call x1, Pallas kernels, body(): pl.pallas_call(kernel, out_shape=(jax.ShapeDtypeStruct((2, 16, 128), F32)...  70.9 us
    unnamed x4, local copies, waits for them, and re-layouts  1.93 us

profile of v3, /device:TPU:1, one launch (start us, length us, event | category | flops | bytes accessed | tf_op | source)
XLA Modules:
  0.0 73.5 jit_solution(13541324636523361375)
XLA Ops:
  0.6 70.9 %green_step.1 = (f32[2,16,128]{2,1,0:T(8,128)}, f32[16,128]{1,0:T(8,128)}) custom-call(f32[2,16,128]{2,1,0:T(8,128)} %orb.1, f32[3,16,128]{2,1,0:T(8,128)} %pts.1, f32[16,128]{1,0:T(8,128)} %qw.1, f32[16,128]{1,0:T(8,128)} %ext.1, f32[32]{0:T(128)} %screening.1, s32[2]{0:T(128)} %level.1, s32[16,27]{1,0:T(8,128)} %near.1), custom_call_target="tpu_custom_call" | custom-call | tf_op jit(solution)/shard_map/green_step/pallas_call | solution.py:444
  71.5 0.0 copy-start
  71.6 1.3 %copy.11 = f32[2,16,128]{2,1,0:T(8,128)} copy(f32[2,16,128]{2,1,0:T(8,128)} %get-tuple-element.4) | data formatting | bytes 32768
  72.9 0.0 copy-done
  72.9 0.6 copy.12
Async XLA Ops:
  71.5 1.3 %copy-start = (f32[16,128]{1,0:T(8,128)S(1)}, f32[16,128]{1,0:T(8,128)}, u32[]{:S(2)}) copy-start(f32[16,128]{1,0:T(8,128)} %get-tuple-element.5) | copy-start | bytes 24580

commit v4 on v3

--- a/solution.py
+++ b/solution.py
@@ -18,9 +18,7 @@
 NODE = [math.cos((2 * a + 1) * math.pi / 8) for a in range(4)]
 OFFSET = [0.5 * (t + 1.0) for t in NODE]
 FAR = 24
-PLANE = 16
-DENSE = FAR + PLANE
-NEAR = 4 * 4 + 8 * 6 + 4 * 9
+NEAR = 4 * 2 + 8 * 3 + 4 * 5
 
 
 def iota(shape, axis):
@@ -118,38 +116,39 @@
 
     rates = [-screening[level[v]] * (1.0 / math.log(2.0)) for v in range(2)]
 
-    def columns(t):
+    def columns(t, carry):
         for k in range(3):
-            TB[k] = jnp.broadcast_to(pts[k, pl.ds(t, 1), :], (128, 128)).T
+            TB[t, k] = jnp.broadcast_to(pts[k, pl.ds(t, 1), :], (128, 128)).T
+        return carry
 
     def green(r2):
         inv = lax.rsqrt(r2)
         s = r2 * inv
         return [(jnp.exp2(s * rate) * inv).astype(BF16) for rate in rates]
 
-    def far_xy():
+    def far_xy(t):
         a, b, c8 = lane // 4 % 4, lane % 4, lane // 16
         gx = (c8 % 4).astype(F32) * SIDE + SIDE * pick(a, OFFSET)
-        dx = TB[0] - gx
+        dx = TB[t, 0] - gx
         for half in range(2):
             gy = (c8 // 4 + 2 * half).astype(F32) * SIDE + SIDE * pick(b, OFFSET)
-            dy = TB[1] - gy
+            dy = TB[t, 1] - gy
             DXY[half] = dx * dx + (dy * dy + SOFTEN)
 
-    def plane_z():
+    def plane_z(t):
         gz = level_of.astype(F32) * SIDE + SIDE * pick(lane % 4, OFFSET)
-        dz = TB[2] - gz
+        dz = TB[t, 2] - gz
         DXY[0] = dz * dz + SOFTEN
         for b in range(4):
-            dy = TB[1] - OFFSET[b]
+            dy = TB[t, 1] - OFFSET[b]
             DXY[1 + b] = dy * dy
 
-    def far_dz2(lev, d):
-        dz = TB[2] - ((g - 1 + lev).astype(F32) * SIDE + SIDE * OFFSET[d])
+    def far_dz2(t, lev, d):
+        dz = TB[t, 2] - ((g - 1 + lev).astype(F32) * SIDE + SIDE * OFFSET[d])
         return dz * dz
 
-    def plane_xz2(a):
-        dx = TB[0] - pick_scalar(a, OFFSET)
+    def plane_xz2(t, a):
+        dx = TB[t, 0] - pick_scalar(a, OFFSET)
         return dx * dx + DXY[0]
 
     def store_green(block, r2):
@@ -158,54 +157,44 @@
 
     def dense(lo, hi):
         def cell(t, carry):
-            columns(t)
-            far_xy()
+            far_xy(t)
 
             def far(lev, c):
                 for d in range(4):
-                    dz2 = far_dz2(lev, d)
+                    dz2 = far_dz2(t, lev, d)
                     for half in range(2):
-                        store_green(t * DENSE + lev * 8 + d * 2 + half, DXY[half] + dz2)
+                        store_green(t * FAR + lev * 8 + d * 2 + half, DXY[half] + dz2)
                 return c
 
             lax.fori_loop(0, 3, far, 0)
-            plane_z()
-
-            def planes(a, c):
-                xz2 = plane_xz2(a)
-                for b in range(4):
-                    store_green(t * DENSE + FAR + a * 4 + b, xz2 + DXY[1 + b])
-                return c
-
-            lax.fori_loop(0, 4, planes, 0)
             return carry
 
         lax.fori_loop(lo, hi, cell, 0)
 
     def near_slot(t, n):
-        cell = near[t, n]
-        return jnp.where(cell >= 0, jnp.clip(cell - 16 * (g - 1), 0, 47), 48)
-
-    def near_r2(slot):
+        cell = near[t, jnp.minimum(n, 26)]
+        live = (cell >= 0) & (n < 27)
+        return jnp.where(live, jnp.clip(cell - 16 * (g - 1), 0, 47), 48)
+
+    def near_r2(t, slot):
         lev, c = slot // 16, slot % 16
         total = None
         for k in range(3):
-            d = TB[k] - PR[lev, k, pl.ds(c, 1), :]
+            d = TB[t, k] - PR[lev, k, pl.ds(c, 1), :]
             total = d * d + SOFTEN if total is None else total + d * d
         return total
 
     def near_green(lo, hi, off):
         def cell(t, off):
-            columns(t)
-            count = near_count(t) // 3
-
-            def triple(p, c):
-                for i in range(3):
-                    for v, values in enumerate(green(near_r2(near_slot(t, 3 * p + i)))):
+            count = (near_count(t) + 5) // 6
+
+            def six(p, c):
+                for i in range(6):
+                    for v, values in enumerate(green(near_r2(t, near_slot(t, 6 * p + i)))):
                         GN[off + p, v, i] = values
                 return c
 
-            lax.fori_loop(0, count, triple, 0)
+            lax.fori_loop(0, count, six, 0)
             return off + count
 
         return lax.fori_loop(lo, hi, cell, off)
@@ -247,14 +236,22 @@
         return carry
 
     lax.fori_loop(0, 16, masks, 0)
-    dense(0, 5)
+    lax.fori_loop(0, 16, columns, 0)
+    dense(0, 6)
     pl.semaphore_wait(barrier, len(partners))
+
+    offset = [0]
+
+    def more(lo, hi):
+        offset[0] = near_green(lo, hi, offset[0])
 
     spread = [copy(D0, RA.at[d - 1], 0, other_z(d)) for d in range(1, 16)]
     begin(spread)
     edge_points = rim(PR, 1)
     begin(edge_points)
-    dense(5, 14)
+    dense(6, 16)
+    finish(edge_points)
+    more(0, 4)
     all_of(RA, 0, other_z(1))
     total = D0[...]
     for d in range(15):
@@ -296,49 +293,42 @@
         for v, part in enumerate(parts):
             ZF[v] = jnp.where(jnp.abs(level_of - g) >= 2, part, 0.0)
 
-    offset = [0]
-
-    def more(lo, hi):
-        offset[0] = near_green(lo, hi, offset[0])
-
     edge_charge = rim(CV, 3)
     begin(edge_charge)
     small = moments([CV.at[1]], MC)
     edge_moments = rim(MC, 5)
     begin(edge_moments)
     send_planes(small, QC, RC, 7)
-    dense(14, 16)
-    finish(edge_points)
-    more(0, 1)
+    more(4, 6)
     finish(edge_charge)
     finish(edge_moments)
 
-    columns(o)
     acc = jnp.zeros((128, 128), F32)
 
     def near_hartree(p, acc):
         for i in range(3):
             slot = near_slot(o, 3 * p + i)
-            acc = acc + lax.rsqrt(near_r2(slot)) * CV[slot // 16, pl.ds(slot % 16, 1), :]
+            acc = acc + lax.rsqrt(near_r2(o, slot)) * CV[slot // 16, pl.ds(slot % 16, 1), :]
         return acc
 
     acc = lax.fori_loop(0, near_count(o) // 3, near_hartree, acc)
-    far_xy()
+    far_xy(o)
 
     def far_hartree(lev, acc):
         for half in range(2):
             mask = FM[o, pl.ds(lev * 2 + half, 1), :]
             for d in range(4):
                 row = MC[lev, half, d : d + 1, :] * mask
-                acc = acc + lax.rsqrt(DXY[half] + far_dz2(lev, d)) * row
+                acc = acc + lax.rsqrt(DXY[half] + far_dz2(o, lev, d)) * row
         return acc
 
     acc = lax.fori_loop(0, 3, far_hartree, acc)
-    plane_z()
+    plane_z(o)
+    more(6, 7)
     take_planes(RC, 7, 1)
 
     def plane_hartree(a, acc):
-        xz2 = plane_xz2(a)
+        xz2 = plane_xz2(o, a)
         for b in range(4):
             acc = acc + lax.rsqrt(xz2 + DXY[1 + b]) * ZF[0, pl.ds(a * 4 + b, 1), :]
         return acc
@@ -346,7 +336,7 @@
     acc = lax.fori_loop(0, 4, plane_hartree, acc)
     HG[0] = jnp.sum(acc.T, axis=0, keepdims=True)
     begin([copy(HG.at[0], HG.at[d], 8, other_z(d)) for d in range(1, 16)])
-    more(1, 11)
+    more(7, 14)
     all_of(HG.at[1:16], 8, other_z(1))
     for d in range(16):
         hart[pl.ds((o + 16 - d) % 16, 1), :] = HG[d]
@@ -360,15 +350,14 @@
     edge_moments = rim(MS, 11)
     begin(edge_moments)
     send_planes(small, QS, RS, 13)
-    more(11, 16)
+    more(14, 16)
 
     def weigh(values, rows):
         total = None
         for value, row in zip(values, rows):
-            wide = jnp.broadcast_to(row, (16, 128)).astype(BF16)
-            term = value.reshape(8, 16, 128) * wide[None]
+            term = value.astype(F32) * row
             total = term if total is None else total + term
-        return total.astype(F32)
+        return total
 
     def local(lo, hi, off):
         def cell(t, off):
@@ -378,29 +367,29 @@
                 for d in range(4):
                     for v in range(2):
                         r = v * 4 + d
-                        at = t * DENSE + lev * 8 + d * 2
+                        at = t * FAR + lev * 8 + d * 2
                         acc[v] = acc[v] + weigh(
                             [G[at, v], G[at + 1, v]],
                             [MS[lev, half, r : r + 1, :] * masks[half] for half in range(2)],
                         )
                 return tuple(acc)
 
-            acc = lax.fori_loop(0, 3, far, (jnp.zeros((8, 16, 128), F32),) * 2)
-            acc = tuple(a.reshape(128, 128) for a in acc)
-            count = near_count(t) // 3
-
-            def triple(p, acc):
-                acc = list(acc)
-                for i in range(3):
-                    slot = near_slot(t, 3 * p + i)
-                    for v in range(2):
-                        row = SV[slot // 16, v, pl.ds(slot % 16, 1), :]
-                        acc[v] = acc[v] + GN[off + p, v, i].astype(F32) * row
-                return tuple(acc)
-
-            acc = lax.fori_loop(0, count, triple, acc)
+            acc = lax.fori_loop(0, 3, far, (jnp.zeros((128, 128), F32),) * 2)
             for v in range(2):
                 ACC[t, v] = acc[v]
+            count = (near_count(t) + 5) // 6
+
+            def six(p, c):
+                slots = [near_slot(t, 6 * p + i) for i in range(6)]
+                for v in range(2):
+                    total = ACC[t, v]
+                    for i, slot in enumerate(slots):
+                        row = SV[slot // 16, v, pl.ds(slot % 16, 1), :]
+                        total = total + GN[off + p, v, i].astype(F32) * row
+                    ACC[t, v] = total
+                return c
+
+            lax.fori_loop(0, count, six, 0)
             return off + count
 
         return lax.fori_loop(lo, hi, cell, off)
@@ -416,16 +405,26 @@
     take_planes(RS, 13, 2)
 
     def update(t, carry):
+        plane_z(t)
+
+        def planes(j, c):
+            total = [ACC[t, v] for v in range(2)]
+            for a in (2 * j, 2 * j + 1):
+                xz2 = plane_xz2(t, a)
+                for b in range(4):
+                    r2 = xz2 + DXY[1 + b]
+                    inv = lax.rsqrt(r2)
+                    s = r2 * inv
+                    for v in range(2):
+                        row = ZF[v, pl.ds(a * 4 + b, 1), :]
+                        total[v] = total[v] + jnp.exp2(s * rates[v]) * (inv * row)
+            for v in range(2):
+                ACC[t, v] = total[v]
+            return c
+
+        lax.fori_loop(0, 2, planes, 0)
         for v in range(2):
-            acc = ACC[t, v]
-            acc = acc.reshape(8, 16, 128)
-            for ab in range(0, PLANE, 2):
-                at = t * DENSE + FAR + ab
-                acc = acc + weigh(
-                    [G[at, v], G[at + 1, v]], [ZF[v, ab : ab + 1, :], ZF[v, ab + 1 : ab + 2, :]]
-                )
-            acc = acc.reshape(128, 128)
-            out[v, pl.ds(t, 1), :] = SCALE * jnp.sum(acc.T, axis=0, keepdims=True)
+            out[v, pl.ds(t, 1), :] = SCALE * jnp.sum(ACC[t, v].T, axis=0, keepdims=True)
         return carry
 
     lax.fori_loop(0, 16, update, 0)
@@ -450,10 +449,10 @@
         in_specs=[vmem] * 4 + [smem] * 3,
         out_specs=(vmem, vmem),
         scratch_shapes=[
-            bf16(16 * DENSE, 2, 128, 128),
-            bf16(NEAR, 2, 3, 128, 128),
+            bf16(16 * FAR, 2, 128, 128),
+            bf16(NEAR, 2, 6, 128, 128),
             f32(16, 2, 128, 128),
-            f32(3, 128, 128),
+            f32(16, 3, 128, 128),
             f32(5, 128, 128),
             f32(4, 3, 16, 128),
             f32(4, 16, 128),

time: 73.7 us -> 72.8 us (0.988)
  Pallas kernels: 70.9 us -> 70 us
    pallas_call x1, Pallas kernels: 70.9 us -> 70 us  [body(): pl.pallas_call(kernel, out_shape=(jax.ShapeDtypeStruct((2, 16, 128), F32)...]
where the time goes in v4:
time: 72.8 us; the launch traced here: 72.6 us
  Pallas kernels  70 us (96%)
  local copies, waits for them, and re-layouts  1.93 us (3%)
    pallas_call x1, Pallas kernels, body(): pl.pallas_call(kernel, out_shape=(jax.ShapeDtypeStruct((2, 16, 128), F32)...  70 us
    unnamed x4, local copies, waits for them, and re-layouts  1.93 us

profile of v4, /device:TPU:1, one launch (start us, length us, event | category | flops | bytes accessed | tf_op | source)
XLA Modules:
  0.0 72.6 jit_solution(1349934315331853989)
XLA Ops:
  0.6 70.0 %green_step.1 = (f32[2,16,128]{2,1,0:T(8,128)}, f32[16,128]{1,0:T(8,128)}) custom-call(f32[2,16,128]{2,1,0:T(8,128)} %orb.1, f32[3,16,128]{2,1,0:T(8,128)} %pts.1, f32[16,128]{1,0:T(8,128)} %qw.1, f32[16,128]{1,0:T(8,128)} %ext.1, f32[32]{0:T(128)} %screening.1, s32[2]{0:T(128)} %level.1, s32[16,27]{1,0:T(8,128)} %near.1), custom_call_target="tpu_custom_call" | custom-call | tf_op jit(solution)/shard_map/green_step/pallas_call | solution.py:443
  70.6 0.0 copy-start
  70.6 1.3 %copy.11 = f32[2,16,128]{2,1,0:T(8,128)} copy(f32[2,16,128]{2,1,0:T(8,128)} %get-tuple-element.4) | data formatting | bytes 32768
  72.0 0.0 copy-done
  72.0 0.6 copy.12
Async XLA Ops:
  70.6 1.3 %copy-start = (f32[16,128]{1,0:T(8,128)S(1)}, f32[16,128]{1,0:T(8,128)}, u32[]{:S(2)}) copy-start(f32[16,128]{1,0:T(8,128)} %get-tuple-element.5) | copy-start | bytes 24580

commit v5 on v3

--- a/solution.py
+++ b/solution.py
@@ -17,10 +17,16 @@
 SIDE = 0.25
 NODE = [math.cos((2 * a + 1) * math.pi / 8) for a in range(4)]
 OFFSET = [0.5 * (t + 1.0) for t in NODE]
-FAR = 24
-PLANE = 16
+FAR = 12
+PLANE = 8
 DENSE = FAR + PLANE
-NEAR = 4 * 4 + 8 * 6 + 4 * 9
+NEAR = 4 * 2 + 8 * 3 + 4 * 5
+
+CORNERS = (0, 3, 12, 15)
+EDGES = (1, 2, 4, 7, 8, 11, 13, 14)
+INNER = (5, 6, 9, 10)
+SIXES = [2 if t in CORNERS else 5 if t in INNER else 3 for t in range(16)]
+FIRST = [sum(SIXES[:t]) for t in range(16)]
 
 
 def iota(shape, axis):
@@ -41,11 +47,24 @@
     return out
 
 
+def pick_int(index, table):
+    out = jnp.int32(table[0])
+    for i in range(1, len(table)):
+        out = jnp.where(index == i, jnp.int32(table[i]), out)
+    return out
+
+
 def select_rows(row, parts):
     out = jnp.where(row == 0, parts[0], parts[1])
     for i in range(2, 4):
         out = jnp.where(row == i, parts[i], out)
     return out
+
+
+def hi_lo(row):
+    r = iota((16, row.shape[1]), 0)
+    rest = row - row.astype(BF16).astype(F32)
+    return jnp.where(r == 0, row, jnp.where(r == 1, rest, 0.0)).astype(BF16)
 
 
 def lagrange(u):
@@ -69,7 +88,7 @@
 
 def kernel(
     orb, pts, qw, ext, screening, level, near, out, hart,
-    G, GN, ACC, TB, DXY, PR, CV, SV, MC, MS, LG, LP, A, AP, D0, RA,
+    G, GN, TB, DXY, GC, DS, FR, VF, VP, PR, CV, SV, MC, MS, LG, LP, A, AP, D0, RA,
     QC, RC, QS, RS, ZF, HG, FM, send, recv,
 ):
     o = lax.axis_index("orb")
@@ -152,39 +171,57 @@
         dx = TB[0] - pick_scalar(a, OFFSET)
         return dx * dx + DXY[0]
 
-    def store_green(block, r2):
+    def store_green(block, half, r2):
         for v, values in enumerate(green(r2)):
-            G[block, v] = values
+            G[block, v, half * 128 : half * 128 + 128, :] = values
+
+    def proxy_columns():
+        r = iota((128, 128), 0)
+        a, b, c8 = r // 4 % 4, r % 4, r // 16
+        GC[0] = (c8 % 4).astype(F32) * SIDE + SIDE * pick(a, OFFSET)
+        for half in range(2):
+            GC[1 + half] = (c8 // 4 + 2 * half).astype(F32) * SIDE + SIDE * pick(b, OFFSET)
+        plane = (g + 32 - (r // 8 + 16 * (r // 4 % 2))) % 32
+        GC[3] = plane.astype(F32) * SIDE + SIDE * pick(r % 4, OFFSET)
 
     def dense(lo, hi):
         def cell(t, carry):
-            columns(t)
-            far_xy()
+            tx, ty, tz = (pts[k, pl.ds(t, 1), :] for k in range(3))
+            dx = tx - GC[0]
+            dx2 = dx * dx + SOFTEN
+            for half in range(2):
+                dy = ty - GC[1 + half]
+                DS[half] = dx2 + dy * dy
+            dz = tz - GC[3]
+            DS[2] = dz * dz + SOFTEN
 
             def far(lev, c):
                 for d in range(4):
-                    dz2 = far_dz2(lev, d)
+                    dz = tz - ((g - 1 + lev).astype(F32) * SIDE + SIDE * OFFSET[d])
                     for half in range(2):
-                        store_green(t * DENSE + lev * 8 + d * 2 + half, DXY[half] + dz2)
+                        store_green(t * DENSE + lev * 4 + d, half, DS[half] + dz * dz)
                 return c
 
             lax.fori_loop(0, 3, far, 0)
-            plane_z()
-
-            def planes(a, c):
-                xz2 = plane_xz2(a)
-                for b in range(4):
-                    store_green(t * DENSE + FAR + a * 4 + b, xz2 + DXY[1 + b])
+
+            def planes(j, c):
+                for i in range(2):
+                    dx = tx - pick_scalar(2 * j + i, OFFSET)
+                    for b in range(4):
+                        dy = ty - OFFSET[b]
+                        at = t * DENSE + FAR + j * 4 + i * 2 + b // 2
+                        store_green(at, b % 2, DS[2] + (dx * dx + dy * dy))
                 return c
 
-            lax.fori_loop(0, 4, planes, 0)
+            lax.fori_loop(0, 2, planes, 0)
             return carry
 
         lax.fori_loop(lo, hi, cell, 0)
 
     def near_slot(t, n):
-        cell = near[t, n]
-        return jnp.where(cell >= 0, jnp.clip(cell - 16 * (g - 1), 0, 47), 48)
+        cell = near[t, jnp.minimum(n, 26)]
+        live = (cell >= 0) & (n < 27)
+        return jnp.where(live, jnp.clip(cell - 16 * (g - 1), 0, 47), 48)
 
     def near_r2(slot):
         lev, c = slot // 16, slot % 16
@@ -197,15 +234,15 @@
     def near_green(lo, hi, off):
         def cell(t, off):
             columns(t)
-            count = near_count(t) // 3
-
-            def triple(p, c):
-                for i in range(3):
-                    for v, values in enumerate(green(near_r2(near_slot(t, 3 * p + i)))):
+            count = (near_count(t) + 5) // 6
+
+            def six(p, c):
+                for i in range(6):
+                    for v, values in enumerate(green(near_r2(near_slot(t, 6 * p + i)))):
                         GN[off + p, v, i] = values
                 return c
 
-            lax.fori_loop(0, count, triple, 0)
+            lax.fori_loop(0, count, six, 0)
             return off + count
 
         return lax.fori_loop(lo, hi, cell, off)
@@ -247,14 +284,22 @@
         return carry
 
     lax.fori_loop(0, 16, masks, 0)
-    dense(0, 5)
+    proxy_columns()
+    dense(0, 4)
     pl.semaphore_wait(barrier, len(partners))
+
+    offset = [0]
+
+    def more(lo, hi):
+        offset[0] = near_green(lo, hi, offset[0])
 
     spread = [copy(D0, RA.at[d - 1], 0, other_z(d)) for d in range(1, 16)]
     begin(spread)
     edge_points = rim(PR, 1)
     begin(edge_points)
-    dense(5, 14)
+    dense(4, 12)
+    finish(edge_points)
+    more(0, 3)
     all_of(RA, 0, other_z(1))
     total = D0[...]
     for d in range(15):
@@ -296,20 +341,14 @@
         for v, part in enumerate(parts):
             ZF[v] = jnp.where(jnp.abs(level_of - g) >= 2, part, 0.0)
 
-    offset = [0]
-
-    def more(lo, hi):
-        offset[0] = near_green(lo, hi, offset[0])
-
     edge_charge = rim(CV, 3)
     begin(edge_charge)
     small = moments([CV.at[1]], MC)
     edge_moments = rim(MC, 5)
     begin(edge_moments)
     send_planes(small, QC, RC, 7)
-    dense(14, 16)
-    finish(edge_points)
-    more(0, 1)
+    dense(12, 14)
+    more(3, 4)
     finish(edge_charge)
     finish(edge_moments)
 
@@ -346,7 +385,7 @@
     acc = lax.fori_loop(0, 4, plane_hartree, acc)
     HG[0] = jnp.sum(acc.T, axis=0, keepdims=True)
     begin([copy(HG.at[0], HG.at[d], 8, other_z(d)) for d in range(1, 16)])
-    more(1, 11)
+    more(4, 12)
     all_of(HG.at[1:16], 8, other_z(1))
     for d in range(16):
         hart[pl.ds((o + 16 - d) % 16, 1), :] = HG[d]
@@ -360,75 +399,72 @@
     edge_moments = rim(MS, 11)
     begin(edge_moments)
     send_planes(small, QS, RS, 13)
-    more(11, 16)
-
-    def weigh(values, rows):
-        total = None
-        for value, row in zip(values, rows):
-            wide = jnp.broadcast_to(row, (16, 128)).astype(BF16)
-            term = value.reshape(8, 16, 128) * wide[None]
-            total = term if total is None else total + term
-        return total.astype(F32)
-
-    def local(lo, hi, off):
-        def cell(t, off):
-            def far(lev, acc):
-                acc = list(acc)
-                masks = [FM[t, pl.ds(lev * 2 + half, 1), :] for half in range(2)]
-                for d in range(4):
-                    for v in range(2):
-                        r = v * 4 + d
-                        at = t * DENSE + lev * 8 + d * 2
-                        acc[v] = acc[v] + weigh(
-                            [G[at, v], G[at + 1, v]],
-                            [MS[lev, half, r : r + 1, :] * masks[half] for half in range(2)],
-                        )
-                return tuple(acc)
-
-            acc = lax.fori_loop(0, 3, far, (jnp.zeros((8, 16, 128), F32),) * 2)
-            acc = tuple(a.reshape(128, 128) for a in acc)
-            count = near_count(t) // 3
-
-            def triple(p, acc):
-                acc = list(acc)
-                for i in range(3):
-                    slot = near_slot(t, 3 * p + i)
-                    for v in range(2):
-                        row = SV[slot // 16, v, pl.ds(slot % 16, 1), :]
-                        acc[v] = acc[v] + GN[off + p, v, i].astype(F32) * row
-                return tuple(acc)
-
-            acc = lax.fori_loop(0, count, triple, acc)
-            for v in range(2):
-                ACC[t, v] = acc[v]
-            return off + count
-
-        return lax.fori_loop(lo, hi, cell, off)
-
-    done = [0]
-
-    def apply(lo, hi):
-        done[0] = local(lo, hi, done[0])
+    more(12, 16)
+    dense(14, 16)
 
     finish(edge_sources)
     finish(edge_moments)
-    apply(0, 16)
+    for v in range(2):
+        for lev in range(3):
+            for d in range(4):
+                r = v * 4 + d
+                rows = [MS[lev, half, r : r + 1, :] for half in range(2)]
+                VF[lev * 4 + d, v] = hi_lo(jnp.concatenate(rows, axis=1))
+
+    def product(rows, block, v):
+        return lax.dot_general(
+            rows, G[block, v], (((1,), (0,)), ((), ())), preferred_element_type=F32
+        )
+
+    def local(cells, sixes):
+        def cell(i, carry):
+            t = pick_int(i, cells)
+            off = pick_int(i, [FIRST[c] for c in cells])
+            far = [jnp.zeros((16, 128), F32) for _ in range(2)]
+            for lev in range(3):
+                mask = jnp.concatenate(
+                    [
+                        jnp.broadcast_to(FM[t, lev * 2 + half : lev * 2 + half + 1, :], (16, 128))
+                        for half in range(2)
+                    ],
+                    axis=1,
+                ).astype(BF16)
+                for d in range(4):
+                    k = lev * 4 + d
+                    for v in range(2):
+                        far[v] = far[v] + product(VF[k, v] * mask, t * DENSE + k, v)
+            slots = [near_slot(t, n) for n in range(6 * sixes)]
+            for v in range(2):
+                total = None
+                for n, slot in enumerate(slots):
+                    row = SV[slot // 16, v, pl.ds(slot % 16, 1), :]
+                    term = GN[off + n // 6, v, n % 6].astype(F32) * row
+                    total = term if total is None else total + term
+                near_row = jnp.sum(total.T, axis=0, keepdims=True)
+                FR[v, pl.ds(t, 1), :] = near_row + (far[v][0:1] + far[v][1:2])
+            return carry
+
+        lax.fori_loop(0, len(cells), cell, 0)
+
+    local(CORNERS, 2)
+    local(EDGES, 3)
+    local(INNER, 5)
     take_planes(RS, 13, 2)
+    for v in range(2):
+        for k in range(PLANE):
+            rows = [ZF[v, 2 * k + half : 2 * k + half + 1, :] for half in range(2)]
+            VP[k, v] = hi_lo(jnp.concatenate(rows, axis=1))
 
     def update(t, carry):
         for v in range(2):
-            acc = ACC[t, v]
-            acc = acc.reshape(8, 16, 128)
-            for ab in range(0, PLANE, 2):
-                at = t * DENSE + FAR + ab
-                acc = acc + weigh(
-                    [G[at, v], G[at + 1, v]], [ZF[v, ab : ab + 1, :], ZF[v, ab + 1 : ab + 2, :]]
-                )
-            acc = acc.reshape(128, 128)
-            out[v, pl.ds(t, 1), :] = SCALE * jnp.sum(acc.T, axis=0, keepdims=True)
+            acc = jnp.zeros((16, 128), F32)
+            for k in range(PLANE):
+                acc = acc + product(VP[k, v], t * DENSE + FAR + k, v)
+            row = FR[v, pl.ds(t, 1), :] + (acc[0:1] + acc[1:2])
+            out[v, pl.ds(t, 1), :] = SCALE * row
         return carry
 
-    lax.fori_loop(0, 16, update, 0)
+    lax.fori_loop(0, 16, update, 0, unroll=2)
 
 
 def body(orbitals, points, quad_weight, external, screening, level_index, near_cells, far_cells):
@@ -450,11 +486,15 @@
         in_specs=[vmem] * 4 + [smem] * 3,
         out_specs=(vmem, vmem),
         scratch_shapes=[
-            bf16(16 * DENSE, 2, 128, 128),
-            bf16(NEAR, 2, 3, 128, 128),
-            f32(16, 2, 128, 128),
+            bf16(16 * DENSE, 2, 256, 128),
+            bf16(NEAR, 2, 6, 128, 128),
             f32(3, 128, 128),
             f32(5, 128, 128),
+            f32(4, 128, 128),
+            f32(3, 128, 128),
+            f32(2, 16, 128),
+            bf16(FAR, 2, 16, 256),
+            bf16(PLANE, 2, 16, 256),
             f32(4, 3, 16, 128),
             f32(4, 16, 128),
             f32(4, 2, 16, 128),

time: 73.7 us -> 68.5 us (0.929)
  Pallas kernels: 70.9 us -> 65.6 us
    pallas_call x1, Pallas kernels: 70.9 us -> 65.6 us  [body(): pl.pallas_call(kernel, out_shape=(jax.ShapeDtypeStruct((2, 16, 128), F32)...]
where the time goes in v5:
time: 68.5 us; the launch traced here: 68.2 us
  Pallas kernels  65.6 us (96%)
  local copies, waits for them, and re-layouts  1.93 us (3%)
    pallas_call x1, Pallas kernels, body(): pl.pallas_call(kernel, out_shape=(jax.ShapeDtypeStruct((2, 16, 128), F32)...  65.6 us
    unnamed x4, local copies, waits for them, and re-layouts  1.93 us

profile of v5, /device:TPU:1, one launch (start us, length us, event | category | flops | bytes accessed | tf_op | source)
XLA Modules:
  0.0 68.2 jit_solution(2234986617802772666)
XLA Ops:
  0.6 65.6 %green_step.1 = (f32[2,16,128]{2,1,0:T(8,128)}, f32[16,128]{1,0:T(8,128)}) custom-call(f32[2,16,128]{2,1,0:T(8,128)} %orb.1, f32[3,16,128]{2,1,0:T(8,128)} %pts.1, f32[16,128]{1,0:T(8,128)} %qw.1, f32[16,128]{1,0:T(8,128)} %ext.1, f32[32]{0:T(128)} %screening.1, s32[2]{0:T(128)} %level.1, s32[16,27]{1,0:T(8,128)} %near.1), custom_call_target="tpu_custom_call" | custom-call | tf_op jit(solution)/shard_map/green_step/pallas_call | solution.py:480
  66.3 0.0 copy-start
  66.3 1.3 %copy.11 = f32[2,16,128]{2,1,0:T(8,128)} copy(f32[2,16,128]{2,1,0:T(8,128)} %get-tuple-element.4) | data formatting | bytes 32768
  67.6 0.0 copy-done
  67.6 0.6 copy.12
Async XLA Ops:
  66.3 1.3 %copy-start = (f32[16,128]{1,0:T(8,128)S(1)}, f32[16,128]{1,0:T(8,128)}, u32[]{:S(2)}) copy-start(f32[16,128]{1,0:T(8,128)} %get-tuple-element.5) | copy-start | bytes 24580

commit v6 on v5

--- a/solution.py
+++ b/solution.py
@@ -20,13 +20,13 @@
 FAR = 12
 PLANE = 8
 DENSE = FAR + PLANE
-NEAR = 4 * 2 + 8 * 3 + 4 * 5
+NEAR = 4 * 12 + 8 * 18 + 4 * 27
 
 CORNERS = (0, 3, 12, 15)
 EDGES = (1, 2, 4, 7, 8, 11, 13, 14)
 INNER = (5, 6, 9, 10)
-SIXES = [2 if t in CORNERS else 5 if t in INNER else 3 for t in range(16)]
-FIRST = [sum(SIXES[:t]) for t in range(16)]
+NEAREST = [12 if t in CORNERS else 27 if t in INNER else 18 for t in range(16)]
+FIRST = [sum(NEAREST[:t]) for t in range(16)]
 
 
 def iota(shape, axis):
@@ -48,7 +48,7 @@
 
 
 def pick_int(index, table):
-    out = jnp.int32(table[0])
+    out = index * 0 + table[0]
     for i in range(1, len(table)):
         out = jnp.where(index == i, jnp.int32(table[i]), out)
     return out
@@ -87,13 +87,14 @@
 
 
 def kernel(
-    orb, pts, qw, ext, screening, level, near, out, hart,
+    orb, pts, qw, ext, screening, level, near, both,
     G, GN, TB, DXY, GC, DS, FR, VF, VP, PR, CV, SV, MC, MS, LG, LP, A, AP, D0, RA,
     QC, RC, QS, RS, ZF, HG, FM, send, recv,
 ):
     o = lax.axis_index("orb")
     g = lax.axis_index("space")
     up, down = (g + 1) % 32, (g + 31) % 32
+    hart = both.at[2]
     lane = iota((1, 128), 1)
     away = lane // 8 + 16 * (lane // 4 % 2)
     level_of = (g + 32 - away) % 32
@@ -219,9 +220,8 @@
         lax.fori_loop(lo, hi, cell, 0)
 
     def near_slot(t, n):
-        cell = near[t, jnp.minimum(n, 26)]
-        live = (cell >= 0) & (n < 27)
-        return jnp.where(live, jnp.clip(cell - 16 * (g - 1), 0, 47), 48)
+        cell = near[t, n]
+        return jnp.where(cell >= 0, jnp.clip(cell - 16 * (g - 1), 0, 47), 48)
 
     def near_r2(slot):
         lev, c = slot // 16, slot % 16
@@ -231,21 +231,19 @@
             total = d * d + SOFTEN if total is None else total + d * d
         return total
 
-    def near_green(lo, hi, off):
-        def cell(t, off):
+    def near_green(cells):
+        count = NEAREST[cells[0]]
+
+        def cell(i, carry):
+            t = pick_int(i, cells)
+            off = pick_int(i, [FIRST[c] for c in cells])
             columns(t)
-            count = (near_count(t) + 5) // 6
-
-            def six(p, c):
-                for i in range(6):
-                    for v, values in enumerate(green(near_r2(near_slot(t, 6 * p + i)))):
-                        GN[off + p, v, i] = values
-                return c
-
-            lax.fori_loop(0, count, six, 0)
-            return off + count
-
-        return lax.fori_loop(lo, hi, cell, off)
+            for n in range(count):
+                for v, values in enumerate(green(near_r2(near_slot(t, n)))):
+                    GN[off + n, v] = values
+            return carry
+
+        lax.fori_loop(0, len(cells), cell, 0)
 
     D0[...] = 2.0 * (orb[0] * orb[0] + orb[1] * orb[1])
     PR[1] = pts[...]
@@ -288,18 +286,13 @@
     dense(0, 4)
     pl.semaphore_wait(barrier, len(partners))
 
-    offset = [0]
-
-    def more(lo, hi):
-        offset[0] = near_green(lo, hi, offset[0])
-
     spread = [copy(D0, RA.at[d - 1], 0, other_z(d)) for d in range(1, 16)]
     begin(spread)
     edge_points = rim(PR, 1)
     begin(edge_points)
     dense(4, 12)
     finish(edge_points)
-    more(0, 3)
+    near_green(CORNERS)
     all_of(RA, 0, other_z(1))
     total = D0[...]
     for d in range(15):
@@ -348,7 +341,7 @@
     begin(edge_moments)
     send_planes(small, QC, RC, 7)
     dense(12, 14)
-    more(3, 4)
+    near_green(INNER[:1])
     finish(edge_charge)
     finish(edge_moments)
 
@@ -385,7 +378,8 @@
     acc = lax.fori_loop(0, 4, plane_hartree, acc)
     HG[0] = jnp.sum(acc.T, axis=0, keepdims=True)
     begin([copy(HG.at[0], HG.at[d], 8, other_z(d)) for d in range(1, 16)])
-    more(4, 12)
+    near_green(EDGES)
+    dense(14, 15)
     all_of(HG.at[1:16], 8, other_z(1))
     for d in range(16):
         hart[pl.ds((o + 16 - d) % 16, 1), :] = HG[d]
@@ -399,8 +393,8 @@
     edge_moments = rim(MS, 11)
     begin(edge_moments)
     send_planes(small, QS, RS, 13)
-    more(12, 16)
-    dense(14, 16)
+    near_green(INNER[1:])
+    dense(15, 16)
 
     finish(edge_sources)
     finish(edge_moments)
@@ -416,7 +410,7 @@
             rows, G[block, v], (((1,), (0,)), ((), ())), preferred_element_type=F32
         )
 
-    def local(cells, sixes):
+    def local(cells):
         def cell(i, carry):
             t = pick_int(i, cells)
             off = pick_int(i, [FIRST[c] for c in cells])
@@ -433,22 +427,22 @@
                     k = lev * 4 + d
                     for v in range(2):
                         far[v] = far[v] + product(VF[k, v] * mask, t * DENSE + k, v)
-            slots = [near_slot(t, n) for n in range(6 * sixes)]
+            slots = [near_slot(t, n) for n in range(NEAREST[cells[0]])]
             for v in range(2):
                 total = None
                 for n, slot in enumerate(slots):
                     row = SV[slot // 16, v, pl.ds(slot % 16, 1), :]
-                    term = GN[off + n // 6, v, n % 6].astype(F32) * row
+                    term = GN[off + n, v].astype(F32) * row
                     total = term if total is None else total + term
                 near_row = jnp.sum(total.T, axis=0, keepdims=True)
                 FR[v, pl.ds(t, 1), :] = near_row + (far[v][0:1] + far[v][1:2])
             return carry
 
-        lax.fori_loop(0, len(cells), cell, 0)
-
-    local(CORNERS, 2)
-    local(EDGES, 3)
-    local(INNER, 5)
+        lax.fori_loop(0, len(cells), cell, 0, unroll=2)
+
+    local(CORNERS)
+    local(EDGES)
+    local(INNER)
     take_planes(RS, 13, 2)
     for v in range(2):
         for k in range(PLANE):
@@ -461,7 +455,7 @@
             for k in range(PLANE):
                 acc = acc + product(VP[k, v], t * DENSE + FAR + k, v)
             row = FR[v, pl.ds(t, 1), :] + (acc[0:1] + acc[1:2])
-            out[v, pl.ds(t, 1), :] = SCALE * row
+            both[v, pl.ds(t, 1), :] = SCALE * row
         return carry
 
     lax.fori_loop(0, 16, update, 0, unroll=2)
@@ -477,17 +471,14 @@
     def bf16(*shape):
         return pltpu.VMEM(shape, BF16)
 
-    return pl.pallas_call(
+    both = pl.pallas_call(
         kernel,
-        out_shape=(
-            jax.ShapeDtypeStruct((2, 16, 128), F32),
-            jax.ShapeDtypeStruct((16, 128), F32),
-        ),
+        out_shape=jax.ShapeDtypeStruct((3, 16, 128), F32),
         in_specs=[vmem] * 4 + [smem] * 3,
-        out_specs=(vmem, vmem),
+        out_specs=vmem,
         scratch_shapes=[
             bf16(16 * DENSE, 2, 256, 128),
-            bf16(NEAR, 2, 6, 128, 128),
+            bf16(NEAR, 2, 128, 128),
             f32(3, 128, 128),
             f32(5, 128, 128),
             f32(4, 128, 128),
@@ -521,6 +512,7 @@
         ),
         name="green_step",
     )(orbitals, points, quad_weight, external, screening, level_index, near_cells)
+    return both[:2], both[2]
 
 
 def solution(mesh):

time: 68.5 us -> 65.7 us (0.959)
  Pallas kernels: 65.6 us -> 62.1 us
  local copies, waits for them, and re-layouts: 1.93 us -> 2.62 us
    pallas_call x1, Pallas kernels: 65.6 us -> 62.1 us  [body(): pl.pallas_call(kernel, out_shape=jax.ShapeDtypeStruct((3, 16, 128), F32),...]
    unnamed x4 -> x0, local copies, waits for them, and re-layouts: 1.93 us -> none
    slice x0 -> x1, local copies, waits for them, and re-layouts: none -> 1.32 us  [body(): return (both[:2], both[2])]
    squeeze x0 -> x1, local copies, waits for them, and re-layouts: none -> 1.3 us  [body(): return (both[:2], both[2])]
where the time goes in v6:
time: 65.7 us; the launch traced here: 65.3 us
  Pallas kernels  62.1 us (95%)
  local copies, waits for them, and re-layouts  2.62 us (4%)
    pallas_call x1, Pallas kernels, body(): pl.pallas_call(kernel, out_shape=jax.ShapeDtypeStruct((3, 16, 128), F32),...  62.1 us
    slice x1, local copies, waits for them, and re-layouts, body(): return (both[:2], both[2])  1.32 us

profile of v6, /device:TPU:1, one launch (start us, length us, event | category | flops | bytes accessed | tf_op | source)
XLA Modules:
  0.0 65.3 jit_solution(7003501539579062541)
XLA Ops:
  0.6 62.1 %green_step.1 = f32[3,16,128]{2,1,0:T(8,128)} custom-call(f32[2,16,128]{2,1,0:T(8,128)} %orb.1, f32[3,16,128]{2,1,0:T(8,128)} %pts.1, f32[16,128]{1,0:T(8,128)} %qw.1, f32[16,128]{1,0:T(8,128)} %ext.1, f32[32]{0:T(128)} %screening.1, s32[2]{0:T(128)} %level.1, s32[16,27]{1,0:T(8,128)} %near.1), custom_call_target="tpu_custom_call" | custom-call | tf_op jit(solution)/shard_map/green_step/pallas_call | solution.py:474
  62.7 1.3 %slice_bitcast_fusion = f32[16,128]{1,0:T(8,128)} fusion(f32[3,16,128]{2,1,0:T(8,128)} %green_step.1), kind=kLoop, calls=%fused_computation | loop fusion | bytes 16384 | tf_op jit(solution)/shard_map/squeeze | solution.py:515
  64.0 1.3 %slice.6 = f32[2,16,128]{2,1,0:T(8,128)} slice(f32[3,16,128]{2,1,0:T(8,128)} %green_step.1), slice={[0:2], [0:16], [0:128]} | slice | bytes 32768 | tf_op jit(solution)/shard_map/slice | solution.py:515

commit v7 on v6

--- a/solution.py
+++ b/solution.py
@@ -87,14 +87,13 @@
 
 
 def kernel(
-    orb, pts, qw, ext, screening, level, near, both,
+    orb, pts, qw, ext, screening, level, near, out, hart,
     G, GN, TB, DXY, GC, DS, FR, VF, VP, PR, CV, SV, MC, MS, LG, LP, A, AP, D0, RA,
     QC, RC, QS, RS, ZF, HG, FM, send, recv,
 ):
     o = lax.axis_index("orb")
     g = lax.axis_index("space")
     up, down = (g + 1) % 32, (g + 31) % 32
-    hart = both.at[2]
     lane = iota((1, 128), 1)
     away = lane // 8 + 16 * (lane // 4 % 2)
     level_of = (g + 32 - away) % 32
@@ -203,7 +202,7 @@
                         store_green(t * DENSE + lev * 4 + d, half, DS[half] + dz * dz)
                 return c
 
-            lax.fori_loop(0, 3, far, 0)
+            lax.fori_loop(0, 3, far, 0, unroll=3)
 
             def planes(j, c):
                 for i in range(2):
@@ -214,7 +213,7 @@
                         store_green(at, b % 2, DS[2] + (dx * dx + dy * dy))
                 return c
 
-            lax.fori_loop(0, 2, planes, 0)
+            lax.fori_loop(0, 2, planes, 0, unroll=2)
             return carry
 
         lax.fori_loop(lo, hi, cell, 0)
@@ -365,7 +364,7 @@
                 acc = acc + lax.rsqrt(DXY[half] + far_dz2(lev, d)) * row
         return acc
 
-    acc = lax.fori_loop(0, 3, far_hartree, acc)
+    acc = lax.fori_loop(0, 3, far_hartree, acc, unroll=3)
     plane_z()
     take_planes(RC, 7, 1)
 
@@ -375,7 +374,7 @@
             acc = acc + lax.rsqrt(xz2 + DXY[1 + b]) * ZF[0, pl.ds(a * 4 + b, 1), :]
         return acc
 
-    acc = lax.fori_loop(0, 4, plane_hartree, acc)
+    acc = lax.fori_loop(0, 4, plane_hartree, acc, unroll=4)
     HG[0] = jnp.sum(acc.T, axis=0, keepdims=True)
     begin([copy(HG.at[0], HG.at[d], 8, other_z(d)) for d in range(1, 16)])
     near_green(EDGES)
@@ -455,7 +454,7 @@
             for k in range(PLANE):
                 acc = acc + product(VP[k, v], t * DENSE + FAR + k, v)
             row = FR[v, pl.ds(t, 1), :] + (acc[0:1] + acc[1:2])
-            both[v, pl.ds(t, 1), :] = SCALE * row
+            out[v, pl.ds(t, 1), :] = SCALE * row
         return carry
 
     lax.fori_loop(0, 16, update, 0, unroll=2)
@@ -471,11 +470,14 @@
     def bf16(*shape):
         return pltpu.VMEM(shape, BF16)
 
-    both = pl.pallas_call(
+    return pl.pallas_call(
         kernel,
-        out_shape=jax.ShapeDtypeStruct((3, 16, 128), F32),
+        out_shape=(
+            jax.ShapeDtypeStruct((2, 16, 128), F32),
+            jax.ShapeDtypeStruct((16, 128), F32),
+        ),
         in_specs=[vmem] * 4 + [smem] * 3,
-        out_specs=vmem,
+        out_specs=(vmem, vmem),
         scratch_shapes=[
             bf16(16 * DENSE, 2, 256, 128),
             bf16(NEAR, 2, 128, 128),
@@ -512,7 +514,6 @@
         ),
         name="green_step",
     )(orbitals, points, quad_weight, external, screening, level_index, near_cells)
-    return both[:2], both[2]
 
 
 def solution(mesh):

time: 65.7 us -> 64.2 us (0.977)
  Pallas kernels: 62.1 us -> 61.4 us
  local copies, waits for them, and re-layouts: 2.62 us -> 1.93 us
    unnamed x0 -> x4, local copies, waits for them, and re-layouts: none -> 1.93 us
    slice x1 -> x0, local copies, waits for them, and re-layouts: 1.32 us -> none  [body(): return (both[:2], both[2])]
    squeeze x1 -> x0, local copies, waits for them, and re-layouts: 1.3 us -> none  [body(): return (both[:2], both[2])]
    pallas_call x1, Pallas kernels: 62.1 us -> 61.4 us  [body(): pl.pallas_call(kernel, out_shape=(jax.ShapeDtypeStruct((2, 16, 128), F32)...]
where the time goes in v7:
time: 64.2 us; the launch traced here: 64 us
  Pallas kernels  61.4 us (96%)
  local copies, waits for them, and re-layouts  1.93 us (3%)
  between operations  0.65 us (1%)
    pallas_call x1, Pallas kernels, body(): pl.pallas_call(kernel, out_shape=(jax.ShapeDtypeStruct((2, 16, 128), F32)...  61.4 us
    unnamed x4, local copies, waits for them, and re-layouts  1.93 us

profile of v7, /device:TPU:1, one launch (start us, length us, event | category | flops | bytes accessed | tf_op | source)
XLA Modules:
  0.0 64.0 jit_solution(15512704232600954632)
XLA Ops:
  0.6 61.4 %green_step.1 = (f32[2,16,128]{2,1,0:T(8,128)}, f32[16,128]{1,0:T(8,128)}) custom-call(f32[2,16,128]{2,1,0:T(8,128)} %orb.1, f32[3,16,128]{2,1,0:T(8,128)} %pts.1, f32[16,128]{1,0:T(8,128)} %qw.1, f32[16,128]{1,0:T(8,128)} %ext.1, f32[32]{0:T(128)} %screening.1, s32[2]{0:T(128)} %level.1, s32[16,27]{1,0:T(8,128)} %near.1), custom_call_target="tpu_custom_call" | custom-call | tf_op jit(solution)/shard_map/green_step/pallas_call | solution.py:473
  62.0 0.0 copy-start
  62.0 1.3 %copy.11 = f32[2,16,128]{2,1,0:T(8,128)} copy(f32[2,16,128]{2,1,0:T(8,128)} %get-tuple-element.4) | data formatting | bytes 32768
  63.4 0.0 copy-done
  63.4 0.6 copy.12
Async XLA Ops:
  62.0 1.3 %copy-start = (f32[16,128]{1,0:T(8,128)S(1)}, f32[16,128]{1,0:T(8,128)}, u32[]{:S(2)}) copy-start(f32[16,128]{1,0:T(8,128)} %get-tuple-element.5) | copy-start | bytes 24580
